TPU v7x, 512 devices: a whole 4x4x16 slice. The times are simulated.
512 devices in a mesh: gx: 32 (over y, x, core), gy: 16 (over z).
Axes of the slice: x: 4, y: 4, z: 16, core: 2. Of those that a mesh axis runs over, the one named last changes fastest.
Arguments:
- test_vectors: float32 [5, 64, 65536], P(None, None, ('gx', 'gy')), may hold values from -1100 to 1100
- face_jacobians: float32 [4, 5, 5], replicated, may hold values from -2.4 to 2.4
- wave_speed: float32 [65536], P(('gx', 'gy')), may hold values from 0.5 to 2
- viscosity: float32 [65536], P(('gx', 'gy')), may hold values from 0.05 to 0.5
- inverse_volume: float32 [65536], P(('gx', 'gy')), may hold values from 0.5 to 2
- connectivity: int32 [4, 65536], P(None, ('gx', 'gy')), may hold values from 0 to 192, as said below
- send_rows: int32 [4, 8192], P(None, ('gx', 'gy')), may hold values from 0 to 127, as said below
- cell_count: int32 [512], P(('gx', 'gy')), may hold values from 64 to 128, as said below
Outputs:
- basis_vectors: float32 [5, 64, 65536], P(None, None, ('gx', 'gy'))
- factor: float32 [64, 64], replicated
Inputs may be any that keep to these rules, and one draw needn't show every extreme that they name: `cell_count`: one partition holds exactly 128 live cells and one exactly 64. `send_rows`: entries of partition p's lists name its owned cells below cell_count[p]; list 0 goes to the partition one row lower, 1 one row higher, 2 one column lower, 3 one column higher; every slot is sent, used or not. `connectivity`: an entry below 128 is a live owned cell; 128 + b * 16 + s is slot s of ghost block b, used only where that neighbouring partition exists; 192 is the far field (zero perturbation). How many slots of a block are used varies by partition and direction.
All inputs are finite; a program needn't handle non-finite values.
Results may differ from a plain program's by a relative error of at most 0.0001.
Values sent between devices are 32-bit elements; how exact they have to be, the bound alone decides.
A program may use at most 64 MiB of HBM per device.

v0:
```python
import jax
import jax.numpy as jnp
from jax import lax
from jax.sharding import PartitionSpec as P

time_step = 0.4


def padded(cells, sides, width):
    for axis, dim in sides:
        count = lax.axis_size(axis)
        ends = count - 1
        head = lax.slice_in_dim(cells, 0, width, axis=dim)
        tail = lax.slice_in_dim(cells, cells.shape[dim] - width, cells.shape[dim], axis=dim)
        cells = jnp.concatenate(
            [
                lax.ppermute(tail, axis, [(i, (i + 1) % count) for i in range(ends)]),
                cells,
                lax.ppermute(head, axis, [((i + 1) % count, i) for i in range(ends)]),
            ],
            axis=dim,
        )
    return cells


def cell_operator(extended, connect, face_jacobians, wave_speed, viscosity, inverse_volume):
    owned_cells = connect.shape[1]
    own_state = extended[:, :, :owned_cells]
    advection = jnp.zeros(own_state.shape, jnp.float32)
    diffusion = jnp.zeros(own_state.shape, jnp.float32)
    for face_index in range(4):
        neighbor = jnp.take(extended, connect[face_index], axis=2)
        advection = advection + jnp.einsum(
            "ij,jvc->ivc", face_jacobians[face_index], neighbor, precision=lax.Precision.HIGHEST
        )
        diffusion = diffusion + neighbor
    return inverse_volume * (
        -0.5 * wave_speed * advection + viscosity * (diffusion - 4.0 * own_state)
    )


def ghost_blocks(current, send_rows):
    outgoing = jnp.moveaxis(jnp.take(current, send_rows, axis=2), 2, 0)
    along_rows = padded(outgoing[0:2], (("gx", 0),), 1)
    along_cols = padded(outgoing[2:4], (("gy", 0),), 1)
    return [along_rows[0], along_rows[3], along_cols[0], along_cols[3]]


def shards(
    test_vectors,
    face_jacobians,
    wave_speed,
    viscosity,
    inverse_volume,
    connectivity,
    send_rows,
    cell_count,
):
    fields, vectors, owned_cells = test_vectors.shape
    speed_cells = wave_speed[None, None, :]
    visc_cells = viscosity[None, None, :]
    volume_cells = inverse_volume[None, None, :]
    zero_block = jnp.zeros((fields, vectors, 1), jnp.float32)

    def operate(state_now):
        incoming = ghost_blocks(state_now, send_rows)
        extended = jnp.concatenate([state_now] + incoming + [zero_block], axis=2)
        return cell_operator(
            extended, connectivity, face_jacobians, speed_cells, visc_cells, volume_cells
        )

    section_one = operate(test_vectors)
    section_two = operate(test_vectors + 0.5 * time_step * section_one)
    section_three = operate(test_vectors + 0.5 * time_step * section_two)
    section_four = operate(test_vectors + time_step * section_three)
    advanced = test_vectors + time_step / 6.0 * (
        section_one + 2.0 * section_two + 2.0 * section_three + section_four
    )
    live_mask = (jnp.arange(owned_cells, dtype=jnp.int32) < cell_count[0]).astype(jnp.float32)
    advanced = advanced * live_mask[None, None, :]
    gram_local = jnp.einsum("fic,fjc->ij", advanced, advanced, precision=lax.Precision.HIGHEST)
    gram_whole = lax.psum(gram_local, ("gx", "gy"))
    total_cells = owned_cells * lax.axis_size("gx") * lax.axis_size("gy")
    gram_whole = gram_whole / float(fields * total_cells)
    lower_factor = jnp.linalg.cholesky(gram_whole)
    inverse_lower = jax.scipy.linalg.solve_triangular(
        lower_factor, jnp.eye(vectors, dtype=jnp.float32), lower=True
    )
    basis_out = jnp.einsum("ij,fjc->fic", inverse_lower, advanced, precision=lax.Precision.HIGHEST)
    return (basis_out, lower_factor.T)


def solution(mesh):
    placed = (
        P(None, None, ("gx", "gy")),
        P(),
        P(("gx", "gy")),
        P(("gx", "gy")),
        P(("gx", "gy")),
        P(None, ("gx", "gy")),
        P(None, ("gx", "gy")),
        P(("gx", "gy")),
    )
    return jax.shard_map(
        shards,
        mesh=mesh,
        in_specs=placed,
        out_specs=(P(None, None, ("gx", "gy")), P()),
        check_vma=False,
    )
```

profile of v0, /device:TPU:1, one launch (start us, length us, event | category | flops | bytes accessed | tf_op | source)
XLA Modules:
  0.0 247.2 jit_solution(7612483933133156070)
XLA Ops:
  0.6 0.7 compare_select_fusion
  1.4 1.2 copy.149
  2.7 0.6 gather_fusion
  3.5 4.5 %collective-permute-start = (f32[1,5,64,16]{2,1,3,0:T(8,128)S(1)}, f32[1,5,64,16]{2,1,3,0:T(8,128)S(1)}, u32[]{:S(2)}, u32[]{:S(2)}) collective-permute-start(f32[1,5,64,16]{2,1,3,0:T(8,128)S(1)} %get-tuple-element.35), channel_id=1, source_target_pairs={{0,16},{16,32},{32,48},{48,64},{64,80},{80,96},{96,112},{112,128},... | collective-permute-start | bytes 61448 | tf_op jit(solution)/shard_map/ppermute | solution.py:17
  8.0 5.5 %collective-permute-start.1 = (f32[1,5,64,16]{2,1,3,0:T(8,128)S(1)}, f32[1,5,64,16]{2,1,3,0:T(8,128)S(1)}, u32[]{:S(2)}, u32[]{:S(2)}) collective-permute-start(f32[1,5,64,16]{2,1,3,0:T(8,128)S(1)} %get-tuple-element.34), channel_id=1, source_target_pairs={{16,0},{32,16},{48,32},{64,48},{80,64},{96,80},{112,96},{128,112},... | collective-permute-start | bytes 61448 | tf_op jit(solution)/shard_map/ppermute | solution.py:19
  13.5 1.3 collective-permute-start.2
  14.8 1.3 collective-permute-start.3
  16.2 0.6 copy-done.4
  16.8 0.6 copy-done.9
  17.6 2.9 %collective-permute-done.3 = f32[1,5,64,16]{2,1,3,0:T(8,128)S(1)} collective-permute-done((f32[1,5,64,16]{2,1,3,0:T(8,128)S(1)}, f32[1,5,64,16]{2,1,3,0:T(8,128)S(1)}, u32[]{:S(2)}, u32[]{:S(2)}) %collective-permute-start.3) | collective-permute-done | bytes 20512 | tf_op jit(solution)/shard_map/ppermute | solution.py:19
  20.5 0.8 gather_fusion.4
  21.5 0.8 gather_fusion.3
  22.5 0.8 gather_fusion.2
  23.6 0.8 gather_fusion.1
  27.1 0.6 gather_fusion.5
  28.4 3.0 %collective-permute-start.4 = (f32[1,5,64,16]{3,1,2,0:T(8,128)S(1)}, f32[1,5,64,16]{3,1,2,0:T(8,128)S(1)}, u32[]{:S(2)}, u32[]{:S(2)}) collective-permute-start(f32[1,5,64,16]{3,1,2,0:T(8,128)S(1)} %get-tuple-element.31), channel_id=1, source_target_pairs={{0,16},{16,32},{32,48},{48,64},{64,80},{80,96},{96,112},{112,128},... | collective-permute-start | bytes 61448 | tf_op jit(solution)/shard_map/ppermute | solution.py:17
  31.4 1.9 collective-permute-start.5
  33.3 3.6 %collective-permute-start.6 = (f32[1,5,64,16]{3,1,2,0:T(8,128)S(1)}, f32[1,5,64,16]{3,1,2,0:T(8,128)S(1)}, u32[]{:S(2)}, u32[]{:S(2)}) collective-permute-start(f32[1,5,64,16]{3,1,2,0:T(8,128)S(1)} %get-tuple-element.29), channel_id=1, source_target_pairs={{0,1},{1,2},{2,3},{3,4},{4,5},{5,6},{6,7},{7,8},{8,9},{9,10},{10,1... | collective-permute-start | bytes 61448 | tf_op jit(solution)/shard_map/ppermute | solution.py:17
  36.9 1.3 collective-permute-start.7
  38.2 0.9 collective-permute-done.5
  39.1 1.3 collective-permute-done.6
  40.4 5.2 %collective-permute-done.7 = f32[1,5,64,16]{3,1,2,0:T(8,128)S(1)} collective-permute-done((f32[1,5,64,16]{3,1,2,0:T(8,128)S(1)}, f32[1,5,64,16]{3,1,2,0:T(8,128)S(1)}, u32[]{:S(2)}, u32[]{:S(2)}) %collective-permute-start.7) | collective-permute-done | bytes 20512 | tf_op jit(solution)/shard_map/ppermute | solution.py:19
  46.4 1.6 gather_fusion.9
  48.0 1.6 gather_fusion.8
  49.6 1.6 gather_fusion.7
  51.1 0.8 gather_fusion.6
  51.9 1.3 copy.171
  53.4 1.2 copy.167
  56.8 0.6 gather_fusion.10
  58.0 6.2 %collective-permute-start.8 = (f32[1,5,64,16]{3,1,2,0:T(8,128)S(1)}, f32[1,5,64,16]{3,1,2,0:T(8,128)S(1)}, u32[]{:S(2)}, u32[]{:S(2)}) collective-permute-start(f32[1,5,64,16]{3,1,2,0:T(8,128)S(1)} %get-tuple-element.27), channel_id=1, source_target_pairs={{0,16},{16,32},{32,48},{48,64},{64,80},{80,96},{96,112},{112,128},... | collective-permute-start | bytes 61448 | tf_op jit(solution)/shard_map/ppermute | solution.py:17
  64.3 1.9 collective-permute-start.9
  66.2 4.9 %collective-permute-start.10 = (f32[1,5,64,16]{3,1,2,0:T(8,128)S(1)}, f32[1,5,64,16]{3,1,2,0:T(8,128)S(1)}, u32[]{:S(2)}, u32[]{:S(2)}) collective-permute-start(f32[1,5,64,16]{3,1,2,0:T(8,128)S(1)} %get-tuple-element.25), channel_id=1, source_target_pairs={{0,1},{1,2},{2,3},{3,4},{4,5},{5,6},{6,7},{7,8},{8,9},{9,10},{10,1... | collective-permute-start | bytes 61448 | tf_op jit(solution)/shard_map/ppermute | solution.py:17
  71.1 1.5 collective-permute-start.11
  73.2 1.1 collective-permute-done.10
  74.4 3.8 %collective-permute-done.11 = f32[1,5,64,16]{3,1,2,0:T(8,128)S(1)} collective-permute-done((f32[1,5,64,16]{3,1,2,0:T(8,128)S(1)}, f32[1,5,64,16]{3,1,2,0:T(8,128)S(1)}, u32[]{:S(2)}, u32[]{:S(2)}) %collective-permute-start.11) | collective-permute-done | bytes 20512 | tf_op jit(solution)/shard_map/ppermute | solution.py:19
  79.0 1.6 gather_fusion.14
  80.6 1.6 gather_fusion.13
  82.2 1.6 gather_fusion.12
  83.7 0.8 gather_fusion.11
  84.5 1.3 copy.183
  86.0 1.2 copy.179
  89.4 0.6 gather_fusion.15
  90.6 6.2 %collective-permute-start.12 = (f32[1,5,64,16]{3,1,2,0:T(8,128)S(1)}, f32[1,5,64,16]{3,1,2,0:T(8,128)S(1)}, u32[]{:S(2)}, u32[]{:S(2)}) collective-permute-start(f32[1,5,64,16]{3,1,2,0:T(8,128)S(1)} %get-tuple-element.23), channel_id=1, source_target_pairs={{0,16},{16,32},{32,48},{48,64},{64,80},{80,96},{96,112},{112,128},... | collective-permute-start | bytes 61448 | tf_op jit(solution)/shard_map/ppermute | solution.py:17
  96.8 1.9 collective-permute-start.13
  98.8 3.5 %collective-permute-start.14 = (f32[1,5,64,16]{3,1,2,0:T(8,128)S(1)}, f32[1,5,64,16]{3,1,2,0:T(8,128)S(1)}, u32[]{:S(2)}, u32[]{:S(2)}) collective-permute-start(f32[1,5,64,16]{3,1,2,0:T(8,128)S(1)} %get-tuple-element.21), channel_id=1, source_target_pairs={{0,1},{1,2},{2,3},{3,4},{4,5},{5,6},{6,7},{7,8},{8,9},{9,10},{10,1... | collective-permute-start | bytes 61448 | tf_op jit(solution)/shard_map/ppermute | solution.py:17
  102.3 1.3 collective-permute-start.15
  103.7 1.2 collective-permute-done.13
  104.8 0.8 collective-permute-done.14
  105.6 4.1 %collective-permute-done.15 = f32[1,5,64,16]{3,1,2,0:T(8,128)S(1)} collective-permute-done((f32[1,5,64,16]{3,1,2,0:T(8,128)S(1)}, f32[1,5,64,16]{3,1,2,0:T(8,128)S(1)}, u32[]{:S(2)}, u32[]{:S(2)}) %collective-permute-start.15) | collective-permute-done | bytes 20512 | tf_op jit(solution)/shard_map/ppermute | solution.py:19
  109.7 0.7 copy-done.3
  110.4 1.4 concatenate.15
  112.3 1.6 gather_fusion.16
  113.8 0.8 gather_fusion.17
  114.6 0.8 gather_fusion.18
  115.4 1.6 gather_fusion.19
  117.0 1.2 copy.189
  119.0 1.2 copy.195
  121.9 111.2 %psum.7 = f32[64,64]{0,1:T(8,128)S(1)} all-reduce(f32[64,64]{0,1:T(8,128)S(1)} %convolution_bitcast_fusion.2), channel_id=1, replica_groups=mesh['gx'=32,'gy'=16] {'gx','gy'}, use_global_device_ids=true, to_apply=%region_0.3 | all-reduce | flops 4096 | bytes 32768 | tf_op jit(solution)/shard_map/psum | solution.py:82
  233.2 5.8 %cholesky.17 = f32[64,64]{1,0:T(8,128)S(1)} custom-call(f32[64,64]{1,0:T(8,128)S(1)} %fusion.99), custom_call_target="Cholesky" | custom-call | tf_op jit(solution)/shard_map/jit(cholesky)/cholesky | solution.py:85
  239.1 0.6 compare_reduce_fusion
  239.8 0.7 fusion.100
  240.4 4.9 %custom-call.7 = f32[1,64,64]{1,2,0:T(8,128)S(1)} custom-call(f32[1,64,64]{2,1,0:T(8,128)S(1)} %get-tuple-element.37), custom_call_target="InvertDiagBlocksLowerTriangular" | custom-call | tf_op jit(solution)/shard_map/jit(_solve_triangular)/triangular_solve | solution.py:86
  245.6 1.0 convolution_bitcast_fusion
  246.5 0.7 copy.202
  (91 shorter events, 15.0 us)
Async XLA Ops:
  0.6 0.8 copy-start.5
  3.5 14.1 %collective-permute-start = (f32[1,5,64,16]{2,1,3,0:T(8,128)S(1)}, f32[1,5,64,16]{2,1,3,0:T(8,128)S(1)}, u32[]{:S(2)}, u32[]{:S(2)}) collective-permute-start(f32[1,5,64,16]{2,1,3,0:T(8,128)S(1)} %get-tuple-element.35), channel_id=1, source_target_pairs={{0,16},{16,32},{32,48},{48,64},{64,80},{80,96},{96,112},{112,128},... | collective-permute-start | bytes 61448 | tf_op jit(solution)/shard_map/ppermute | solution.py:17
  8.0 9.6 %collective-permute-start.1 = (f32[1,5,64,16]{2,1,3,0:T(8,128)S(1)}, f32[1,5,64,16]{2,1,3,0:T(8,128)S(1)}, u32[]{:S(2)}, u32[]{:S(2)}) collective-permute-start(f32[1,5,64,16]{2,1,3,0:T(8,128)S(1)} %get-tuple-element.34), channel_id=1, source_target_pairs={{16,0},{32,16},{48,32},{64,48},{80,64},{96,80},{112,96},{128,112},... | collective-permute-start | bytes 61448 | tf_op jit(solution)/shard_map/ppermute | solution.py:19
  13.5 4.1 %collective-permute-start.2 = (f32[1,5,64,16]{2,1,3,0:T(8,128)S(1)}, f32[1,5,64,16]{2,1,3,0:T(8,128)S(1)}, u32[]{:S(2)}, u32[]{:S(2)}) collective-permute-start(f32[1,5,64,16]{2,1,3,0:T(8,128)S(1)} %get-tuple-element.33), channel_id=1, source_target_pairs={{0,1},{1,2},{2,3},{3,4},{4,5},{5,6},{6,7},{7,8},{8,9},{9,10},{10,1... | collective-permute-start | bytes 61448 | tf_op jit(solution)/shard_map/ppermute | solution.py:17
  14.8 1.4 copy-start.8
  14.8 5.7 %collective-permute-start.3 = (f32[1,5,64,16]{2,1,3,0:T(8,128)S(1)}, f32[1,5,64,16]{2,1,3,0:T(8,128)S(1)}, u32[]{:S(2)}, u32[]{:S(2)}) collective-permute-start(f32[1,5,64,16]{2,1,3,0:T(8,128)S(1)} %get-tuple-element.32), channel_id=1, source_target_pairs={{1,0},{2,1},{3,2},{4,3},{5,4},{6,5},{7,6},{8,7},{9,8},{10,9},{11,1... | collective-permute-start | bytes 61448 | tf_op jit(solution)/shard_map/ppermute | solution.py:19
  16.1 0.7 copy-start.4
  16.8 0.7 copy-start.9
  25.3 0.9 copy-start
  25.7 0.7 copy-start.6
  25.7 0.7 copy-start.7
  28.4 9.8 %collective-permute-start.4 = (f32[1,5,64,16]{3,1,2,0:T(8,128)S(1)}, f32[1,5,64,16]{3,1,2,0:T(8,128)S(1)}, u32[]{:S(2)}, u32[]{:S(2)}) collective-permute-start(f32[1,5,64,16]{3,1,2,0:T(8,128)S(1)} %get-tuple-element.31), channel_id=1, source_target_pairs={{0,16},{16,32},{32,48},{48,64},{64,80},{80,96},{96,112},{112,128},... | collective-permute-start | bytes 61448 | tf_op jit(solution)/shard_map/ppermute | solution.py:17
  31.4 7.7 %collective-permute-start.5 = (f32[1,5,64,16]{3,1,2,0:T(8,128)S(1)}, f32[1,5,64,16]{3,1,2,0:T(8,128)S(1)}, u32[]{:S(2)}, u32[]{:S(2)}) collective-permute-start(f32[1,5,64,16]{3,1,2,0:T(8,128)S(1)} %get-tuple-element.30), channel_id=1, source_target_pairs={{16,0},{32,16},{48,32},{64,48},{80,64},{96,80},{112,96},{128,112},... | collective-permute-start | bytes 61448 | tf_op jit(solution)/shard_map/ppermute | solution.py:19
  33.3 7.0 %collective-permute-start.6 = (f32[1,5,64,16]{3,1,2,0:T(8,128)S(1)}, f32[1,5,64,16]{3,1,2,0:T(8,128)S(1)}, u32[]{:S(2)}, u32[]{:S(2)}) collective-permute-start(f32[1,5,64,16]{3,1,2,0:T(8,128)S(1)} %get-tuple-element.29), channel_id=1, source_target_pairs={{0,1},{1,2},{2,3},{3,4},{4,5},{5,6},{6,7},{7,8},{8,9},{9,10},{10,1... | collective-permute-start | bytes 61448 | tf_op jit(solution)/shard_map/ppermute | solution.py:17
  36.9 8.7 %collective-permute-start.7 = (f32[1,5,64,16]{3,1,2,0:T(8,128)S(1)}, f32[1,5,64,16]{3,1,2,0:T(8,128)S(1)}, u32[]{:S(2)}, u32[]{:S(2)}) collective-permute-start(f32[1,5,64,16]{3,1,2,0:T(8,128)S(1)} %get-tuple-element.28), channel_id=1, source_target_pairs={{1,0},{2,1},{3,2},{4,3},{5,4},{6,5},{7,6},{8,7},{9,8},{10,9},{11,1... | collective-permute-start | bytes 61448 | tf_op jit(solution)/shard_map/ppermute | solution.py:19
  51.9 1.3 copy-start.1
  58.0 15.2 %collective-permute-start.8 = (f32[1,5,64,16]{3,1,2,0:T(8,128)S(1)}, f32[1,5,64,16]{3,1,2,0:T(8,128)S(1)}, u32[]{:S(2)}, u32[]{:S(2)}) collective-permute-start(f32[1,5,64,16]{3,1,2,0:T(8,128)S(1)} %get-tuple-element.27), channel_id=1, source_target_pairs={{0,16},{16,32},{32,48},{48,64},{64,80},{80,96},{96,112},{112,128},... | collective-permute-start | bytes 61448 | tf_op jit(solution)/shard_map/ppermute | solution.py:17
  64.3 8.9 %collective-permute-start.9 = (f32[1,5,64,16]{3,1,2,0:T(8,128)S(1)}, f32[1,5,64,16]{3,1,2,0:T(8,128)S(1)}, u32[]{:S(2)}, u32[]{:S(2)}) collective-permute-start(f32[1,5,64,16]{3,1,2,0:T(8,128)S(1)} %get-tuple-element.26), channel_id=1, source_target_pairs={{16,0},{32,16},{48,32},{64,48},{80,64},{96,80},{112,96},{128,112},... | collective-permute-start | bytes 61448 | tf_op jit(solution)/shard_map/ppermute | solution.py:19
  66.2 8.2 %collective-permute-start.10 = (f32[1,5,64,16]{3,1,2,0:T(8,128)S(1)}, f32[1,5,64,16]{3,1,2,0:T(8,128)S(1)}, u32[]{:S(2)}, u32[]{:S(2)}) collective-permute-start(f32[1,5,64,16]{3,1,2,0:T(8,128)S(1)} %get-tuple-element.25), channel_id=1, source_target_pairs={{0,1},{1,2},{2,3},{3,4},{4,5},{5,6},{6,7},{7,8},{8,9},{9,10},{10,1... | collective-permute-start | bytes 61448 | tf_op jit(solution)/shard_map/ppermute | solution.py:17
  71.1 7.1 %collective-permute-start.11 = (f32[1,5,64,16]{3,1,2,0:T(8,128)S(1)}, f32[1,5,64,16]{3,1,2,0:T(8,128)S(1)}, u32[]{:S(2)}, u32[]{:S(2)}) collective-permute-start(f32[1,5,64,16]{3,1,2,0:T(8,128)S(1)} %get-tuple-element.24), channel_id=1, source_target_pairs={{1,0},{2,1},{3,2},{4,3},{5,4},{6,5},{7,6},{8,7},{9,8},{10,9},{11,1... | collective-permute-start | bytes 61448 | tf_op jit(solution)/shard_map/ppermute | solution.py:19
  84.5 1.3 copy-start.2
  90.6 13.0 %collective-permute-start.12 = (f32[1,5,64,16]{3,1,2,0:T(8,128)S(1)}, f32[1,5,64,16]{3,1,2,0:T(8,128)S(1)}, u32[]{:S(2)}, u32[]{:S(2)}) collective-permute-start(f32[1,5,64,16]{3,1,2,0:T(8,128)S(1)} %get-tuple-element.23), channel_id=1, source_target_pairs={{0,16},{16,32},{32,48},{48,64},{64,80},{80,96},{96,112},{112,128},... | collective-permute-start | bytes 61448 | tf_op jit(solution)/shard_map/ppermute | solution.py:17
  96.8 8.0 %collective-permute-start.13 = (f32[1,5,64,16]{3,1,2,0:T(8,128)S(1)}, f32[1,5,64,16]{3,1,2,0:T(8,128)S(1)}, u32[]{:S(2)}, u32[]{:S(2)}) collective-permute-start(f32[1,5,64,16]{3,1,2,0:T(8,128)S(1)} %get-tuple-element.22), channel_id=1, source_target_pairs={{16,0},{32,16},{48,32},{64,48},{80,64},{96,80},{112,96},{128,112},... | collective-permute-start | bytes 61448 | tf_op jit(solution)/shard_map/ppermute | solution.py:19
  98.8 6.8 %collective-permute-start.14 = (f32[1,5,64,16]{3,1,2,0:T(8,128)S(1)}, f32[1,5,64,16]{3,1,2,0:T(8,128)S(1)}, u32[]{:S(2)}, u32[]{:S(2)}) collective-permute-start(f32[1,5,64,16]{3,1,2,0:T(8,128)S(1)} %get-tuple-element.21), channel_id=1, source_target_pairs={{0,1},{1,2},{2,3},{3,4},{4,5},{5,6},{6,7},{7,8},{8,9},{9,10},{10,1... | collective-permute-start | bytes 61448 | tf_op jit(solution)/shard_map/ppermute | solution.py:17
  102.3 7.4 %collective-permute-start.15 = (f32[1,5,64,16]{3,1,2,0:T(8,128)S(1)}, f32[1,5,64,16]{3,1,2,0:T(8,128)S(1)}, u32[]{:S(2)}, u32[]{:S(2)}) collective-permute-start(f32[1,5,64,16]{3,1,2,0:T(8,128)S(1)} %get-tuple-element.20), channel_id=1, source_target_pairs={{1,0},{2,1},{3,2},{4,3},{5,4},{6,5},{7,6},{8,7},{9,8},{10,9},{11,1... | collective-permute-start | bytes 61448 | tf_op jit(solution)/shard_map/ppermute | solution.py:19
  109.7 0.7 copy-start.3
where the time goes:
time: 248 us; the launch traced here: 247 us
  blocking collectives  111 us (45%)
  starting transfers between devices  49.9 us (20%)
  local copies, waits for them, and re-layouts  41.5 us (17%)
  waiting for transfers between devices  21.3 us (9%)
  other arithmetic  13.3 us (5%)
  matrix products  7.87 us (3%)
    psum x1, blocking collectives, shards(): gram_whole = lax.psum(gram_local, ('gx', 'gy'))  111 us
    ppermute x8, starting transfers between devices, padded(): lax.ppermute(tail, axis, [(i, (i + 1) % count) for i in range(ends)])  33.2 us
    gather x32, local copies, waits for them, and re-layouts, cell_operator(): neighbor = jnp.take(extended, connect[face_index], axis=2)  28.5 us
    ppermute x8, waiting for transfers between devices, padded(): lax.ppermute(head, axis, [((i + 1) % count, i) for i in range(ends)])  18.1 us
    ppermute x8, starting transfers between devices, padded(): lax.ppermute(head, axis, [((i + 1) % count, i) for i in range(ends)])  16.7 us
    another operation x3, other arithmetic, shards(): lower_factor = jnp.linalg.cholesky(gram_whole)  6.52 us
    dot_general x16, matrix products, cell_operator(): jnp.einsum('ij,jvc->ivc', face_jacobians[face_index], neighbor, precision...  6.35 us
  transfers between devices with their start and end apart: 16, of which 9 were waited for; matrix products, arithmetic and copies ran while one was open for 0% of the time, Pallas kernels for 0%

commit v1 on v0

v1 whole, which is shorter than its diff:
```python
import functools

import jax
import jax.numpy as jnp
from jax import lax
from jax.experimental import pallas as pl
from jax.experimental.pallas import tpu as pltpu
from jax.sharding import PartitionSpec as P

time_step = 0.4
F32 = jnp.float32
HIGHEST = lax.Precision.HIGHEST
MESH = pl.DeviceIdType.MESH


def pick(x, idx):
    return jnp.take_along_axis(x, idx, axis=1, mode="promise_in_bounds")


def step_kernel(
    nx,
    ny,
    tv_ref,
    fj_ref,
    ws_ref,
    vi_ref,
    iv_ref,
    cn_ref,
    sr_ref,
    cc_ref,
    adv_ref,
    gram_ref,
    w_ref,
    acc_ref,
    pad_ref,
    send_ref,
    recv_ref,
    rows_ref,
    part_ref,
    mine_ref,
    line_ref,
    done_ref,
    whole_ref,
    halo_send_sem,
    halo_recv_sem,
    scat_send_sem,
    scat_recv_sem,
    line_send_sem,
    line_recv_sem,
    gath_send_sem,
    gath_recv_sem,
):
    gx = lax.axis_index("gx")
    gy = lax.axis_index("gy")

    barrier = pltpu.get_barrier_semaphore()

    def greet_x(o, c):
        pl.semaphore_signal(
            barrier, inc=1, device_id=(lax.rem(gx + o, nx), gy), device_id_type=MESH
        )
        return c

    def greet_y(o, c):
        pl.semaphore_signal(
            barrier, inc=1, device_id=(gx, lax.rem(gy + o, ny)), device_id_type=MESH
        )
        return c

    lax.fori_loop(1, nx, greet_x, 0)
    lax.fori_loop(1, ny, greet_y, 0)

    rows = lax.broadcasted_iota(jnp.int32, (64, 128), 0)
    lanes = lax.broadcasted_iota(jnp.int32, (64, 128), 1)
    lanes8 = lax.broadcasted_iota(jnp.int32, (8, 128), 1)
    group8 = lanes8 >> 4
    turn = ((lanes >> 4) - (rows >> 3)) & 7
    listed = turn >> 1
    spare = (turn & 1) == 1

    pad_ref[...] = jnp.zeros_like(pad_ref)
    pad_ref[0:4, 0:16] = sr_ref[...]
    send_tile = pick(pad_ref[...], lanes8 & 15)
    send_idx = jnp.zeros((64, 128), jnp.int32)
    for k in range(4):
        row = jnp.broadcast_to(send_tile[k : k + 1, :], (64, 128))
        send_idx = jnp.where(listed == k, row, send_idx)

    a_row = -0.5 * ws_ref[...] * iv_ref[...]
    b_row = vi_ref[...] * iv_ref[...]

    w_ref[...] = tv_ref[...]

    pl.semaphore_wait(barrier, nx + ny - 2)

    def halo(s, k):
        step = 1 if k % 2 else -1
        there = (gx + step, gy) if k < 2 else (gx, gy + step)
        return pltpu.make_async_remote_copy(
            src_ref=send_ref.at[s, k],
            dst_ref=recv_ref.at[s, k],
            send_sem=halo_send_sem.at[s, k],
            recv_sem=halo_recv_sem.at[s, k],
            device_id=there,
            device_id_type=MESH,
        )

    sends_to = [gx > 0, gx < nx - 1, gy > 0, gy < ny - 1]
    comes_in = [gx < nx - 1, gx > 0, gy < ny - 1, gy > 0]

    def stage(s, carry):
        scale = jnp.where(
            s == 0,
            F32(time_step / 4),
            jnp.where(s == 1, F32(time_step / 3), jnp.where(s == 2, F32(time_step / 2), F32(time_step))),
        )
        a_fac = jnp.broadcast_to(a_row * scale, (64, 128))
        b_fac = jnp.broadcast_to(b_row * scale, (64, 128))
        for j in range(5):
            x = pick(w_ref[j], send_idx)
            for k in range(4):
                out = x[0:8]
                for g in range(1, 8):
                    out = jnp.where(group8 == (g + 2 * k) % 8, x[8 * g : 8 * g + 8], out)
                send_ref[s, k, j] = out
        for k in range(4):

            @pl.when(sends_to[k])
            def _(k=k):
                halo(s, k).start()

        adv = [None] * 5
        dif = [None] * 5
        for f in range(4):
            conn = jnp.broadcast_to(cn_ref[f : f + 1, :], (64, 128))
            own = conn < 128
            idx = conn & 127
            for j in range(5):
                n = jnp.where(own, pick(w_ref[j], idx), 0.0)
                dif[j] = n if f == 0 else dif[j] + n
                for i in range(5):
                    t = fj_ref[f, i, j] * n
                    adv[i] = t if adv[i] is None else adv[i] + t
        for i in range(5):
            acc_ref[i] = tv_ref[i] + a_fac * adv[i] + b_fac * (dif[i] - 4.0 * w_ref[i])

        for k in range(4):

            @pl.when(comes_in[k])
            def _(k=k):
                halo(s, k).wait_recv()

        adv = [None] * 5
        dif = [None] * 5
        for j in range(5):
            ghost = jnp.zeros((64, 128), F32)
            for k in range(4):
                block = jnp.concatenate([recv_ref[s, k, j]] * 8, axis=0)
                ghost = jnp.where(jnp.logical_and(listed == k, jnp.logical_not(spare)), block, ghost)
            for f in range(4):
                conn = jnp.broadcast_to(cn_ref[f : f + 1, :], (64, 128))
                slot = conn - 128
                there = ((rows >> 3) << 4) + (((slot >> 4) ^ 1) << 5) + (slot & 15)
                empty = ((rows >> 3) << 4) + 16
                ours = jnp.logical_and(conn >= 128, conn < 192)
                idx = jnp.where(ours, there, empty) & 127
                n = pick(ghost, idx)
                dif[j] = n if f == 0 else dif[j] + n
                for i in range(5):
                    t = fj_ref[f, i, j] * n
                    adv[i] = t if adv[i] is None else adv[i] + t
        for i in range(5):
            w_ref[i] = acc_ref[i] + (a_fac * adv[i] + b_fac * dif[i])
        return carry

    lax.fori_loop(0, 4, stage, 0)

    live = lanes < cc_ref[0]
    adv = [jnp.where(live, w_ref[j], 0.0) for j in range(5)]
    for j in range(5):
        adv_ref[j] = adv[j]
    flat = jnp.concatenate(adv, axis=1)
    twice = jnp.concatenate([flat, flat], axis=0)
    low = lax.dot_general(flat[0:32], twice, (((1,), (1,)), ((), ())), precision=HIGHEST, preferred_element_type=F32)
    high = lax.dot_general(flat[32:64], twice, (((1,), (1,)), ((), ())), precision=HIGHEST, preferred_element_type=F32)
    lanes32 = lax.broadcasted_iota(jnp.int32, (32, 128), 1)
    packed = jnp.where(lanes32 < 64, low, high)
    for r in range(32):
        rows_ref[r] = packed[r : r + 1]

    per = 32 // nx

    def scatter(o):
        to = lax.rem(gx + o, nx)
        return pltpu.make_async_remote_copy(
            src_ref=rows_ref.at[pl.ds(to * per, per)],
            dst_ref=part_ref.at[nx - o],
            send_sem=scat_send_sem,
            recv_sem=scat_recv_sem,
            device_id=(to, gy),
            device_id_type=MESH,
        )

    def scatter_start(o, c):
        scatter(o).start()
        return c

    lax.fori_loop(1, nx, scatter_start, 0)
    part_ref[0] = rows_ref[pl.ds(gx * per, per)]
    sized = part_ref.at[pl.ds(1, nx - 1)]
    pltpu.make_async_copy(sized, sized, scat_recv_sem).wait()
    total = part_ref[0]
    for o in range(1, nx):
        total = total + part_ref[o]
    mine_ref[...] = total

    def line(o):
        return pltpu.make_async_remote_copy(
            src_ref=mine_ref,
            dst_ref=line_ref.at[ny - o],
            send_sem=line_send_sem,
            recv_sem=line_recv_sem,
            device_id=(gx, lax.rem(gy + o, ny)),
            device_id_type=MESH,
        )

    def line_start(o, c):
        line(o).start()
        return c

    lax.fori_loop(1, ny, line_start, 0)
    line_ref[0] = total
    sized_line = line_ref.at[pl.ds(1, ny - 1)]
    pltpu.make_async_copy(sized_line, sized_line, line_recv_sem).wait()
    total = line_ref[lax.rem(ny - gy, ny)]
    for z in range(1, ny):
        total = total + line_ref[lax.rem(ny + z - gy, ny)]
    total = total / F32(5 * 128 * nx * ny)
    done_ref[...] = total

    def gather(o):
        return pltpu.make_async_remote_copy(
            src_ref=done_ref,
            dst_ref=whole_ref.at[pl.ds(gx * per, per)],
            send_sem=gath_send_sem,
            recv_sem=gath_recv_sem,
            device_id=(lax.rem(gx + o, nx), gy),
            device_id_type=MESH,
        )

    def gather_start(o, c):
        gather(o).start()
        return c

    lax.fori_loop(1, nx, gather_start, 0)
    whole_ref[pl.ds(gx * per, per)] = total
    sized_whole = whole_ref.at[pl.ds(0, 32 - per)]
    pltpu.make_async_copy(sized_whole, sized_whole, gath_recv_sem).wait()
    for r in range(32):
        gram_ref[r : r + 1, :] = whole_ref[r]

    for s in range(4):
        for k in range(4):

            @pl.when(sends_to[k])
            def _(s=s, k=k):
                halo(s, k).wait_send()

    pltpu.make_async_copy(sized, sized, scat_send_sem).wait()
    pltpu.make_async_copy(sized_line, sized_line, line_send_sem).wait()
    pltpu.make_async_copy(sized_whole, sized_whole, gath_send_sem).wait()


def factor_kernel(adv_ref, gram_ref, basis_ref, factor_ref):
    lanes = lax.broadcasted_iota(jnp.int32, (8, 128), 1)
    subs = lax.broadcasted_iota(jnp.int32, (8, 128), 0)
    left = lanes < 64
    a = []
    for p in range(8):
        g = gram_ref[8 * (p % 4) : 8 * (p % 4) + 8, :]
        if p >= 4:
            g = pltpu.roll(g, 64, axis=1)
        unit = jnp.where(lanes - 64 == subs + 8 * p, 1.0, 0.0).astype(F32)
        a.append(jnp.where(left, g, unit))

    def across(x, c):
        return jnp.broadcast_to(x[:, c : c + 1], (8, 128))

    def down(x, r):
        return jnp.broadcast_to(x[r : r + 1, :], (8, 128))

    done = []
    for p in range(8):
        cols = [[across(a[r], 8 * p + j) for r in range(p, 8)] for j in range(8)]
        pivots = jnp.ones((8, 128), F32)
        for k in range(8):
            row_of = [down(cols[j][0], k) if j >= k else None for j in range(8)]
            pivots = jnp.where(subs == k, row_of[k], pivots)
            inverse = 1.0 / row_of[k]
            whole_row = down(a[p], k)
            for r in range(p, 8):
                m = cols[k][r - p] * inverse
                if r == p:
                    m = jnp.where(subs > k, m, 0.0)
                for j in range(k + 1, 8):
                    cols[j][r - p] = cols[j][r - p] - m * row_of[j]
                a[r] = a[r] - m * whole_row
        done.append(a[p] / jnp.sqrt(pivots))

    both = jnp.concatenate(done, axis=0)
    swapped = pltpu.roll(both, 64, axis=1)
    rows = lax.broadcasted_iota(jnp.int32, (64, 64), 0)
    columns = lax.broadcasted_iota(jnp.int32, (64, 64), 1)
    factor_ref[...] = jnp.where(columns >= rows, both[:, 0:64], 0.0)
    inv = swapped[:, 0:64]
    for j in range(5):
        basis_ref[j] = lax.dot_general(
            inv, adv_ref[j], (((1,), (0,)), ((), ())), precision=HIGHEST, preferred_element_type=F32
        )


def shards(tv, fj, ws, vi, iv, cn, sr, cc):
    nx = lax.axis_size("gx")
    ny = lax.axis_size("gy")
    vmem = pl.BlockSpec(memory_space=pltpu.VMEM)
    smem = pl.BlockSpec(memory_space=pltpu.SMEM)
    per = 32 // nx
    adv, gram = pl.pallas_call(
        functools.partial(step_kernel, nx, ny),
        out_shape=(
            jax.ShapeDtypeStruct((5, 64, 128), F32),
            jax.ShapeDtypeStruct((32, 128), F32),
        ),
        in_specs=[vmem, smem, vmem, vmem, vmem, vmem, vmem, smem],
        out_specs=(vmem, vmem),
        scratch_shapes=[
            pltpu.VMEM((5, 64, 128), F32),
            pltpu.VMEM((5, 64, 128), F32),
            pltpu.VMEM((8, 128), jnp.int32),
            pltpu.VMEM((4, 4, 5, 8, 128), F32),
            pltpu.VMEM((4, 4, 5, 8, 128), F32),
            pltpu.VMEM((32, 1, 128), F32),
            pltpu.VMEM((nx, per, 1, 128), F32),
            pltpu.VMEM((per, 1, 128), F32),
            pltpu.VMEM((ny, per, 1, 128), F32),
            pltpu.VMEM((per, 1, 128), F32),
            pltpu.VMEM((32, 1, 128), F32),
            pltpu.SemaphoreType.DMA((4, 4)),
            pltpu.SemaphoreType.DMA((4, 4)),
            pltpu.SemaphoreType.DMA,
            pltpu.SemaphoreType.DMA,
            pltpu.SemaphoreType.DMA,
            pltpu.SemaphoreType.DMA,
            pltpu.SemaphoreType.DMA,
            pltpu.SemaphoreType.DMA,
        ],
        compiler_params=pltpu.CompilerParams(collective_id=0, has_side_effects=True),
        name="advance_and_gram",
    )(tv, fj, ws.reshape(1, 128), vi.reshape(1, 128), iv.reshape(1, 128), cn, sr, cc)
    return pl.pallas_call(
        factor_kernel,
        out_shape=(
            jax.ShapeDtypeStruct((5, 64, 128), F32),
            jax.ShapeDtypeStruct((64, 64), F32),
        ),
        in_specs=[vmem, vmem],
        out_specs=(vmem, vmem),
        name="factor_and_apply",
    )(adv, gram)


def solution(mesh):
    cells = P(("gx", "gy"))
    placed = (
        P(None, None, ("gx", "gy")),
        P(),
        cells,
        cells,
        cells,
        P(None, ("gx", "gy")),
        P(None, ("gx", "gy")),
        cells,
    )
    return jax.shard_map(
        shards,
        mesh=mesh,
        in_specs=placed,
        out_specs=(P(None, None, ("gx", "gy")), P()),
        check_vma=False,
    )
```

time: 248 us -> 59.1 us (0.24)
  blocking collectives: 111 us -> 0 us
  Pallas kernels: 0 us -> 56.3 us
  starting transfers between devices: 49.9 us -> 0 us
  local copies, waits for them, and re-layouts: 41.5 us -> 1.31 us
  waiting for transfers between devices: 21.3 us -> 0 us
  other arithmetic: 13.3 us -> 0 us
  matrix products: 7.87 us -> 0 us
    psum x1 -> x0, blocking collectives: 111 us -> none  [shards(): gram_whole = lax.psum(gram_local, ('gx', 'gy'))]
    pallas_call x0 -> x2, Pallas kernels: none -> 56.3 us  [the longest x1 52.6 us: shards(): pl.pallas_call(functools.partial(step_kernel, nx, ny), out_shape=(jax.Sha...]
    ppermute x16 -> x0, starting transfers between devices: 49.9 us -> none  [the longest x8 33.2 us: padded(): lax.ppermute(tail, axis, [(i, (i + 1) % count) for i in range(ends)])]
    gather x39 -> x0, local copies, waits for them, and re-layouts: 32.2 us -> none  [the longest x32 28.5 us: cell_operator(): neighbor = jnp.take(extended, connect[face_index], axis=2)]
    ppermute x16 -> x0, waiting for transfers between devices: 21.3 us -> none  [the longest x8 18.1 us: padded(): lax.ppermute(head, axis, [((i + 1) % count, i) for i in range(ends)])]
    another operation x4 -> x0, other arithmetic: 11.4 us -> none  [the longest x3 6.52 us: shards(): lower_factor = jnp.linalg.cholesky(gram_whole)]
    dot_general x18 -> x0, matrix products: 7.64 us -> none  [the longest x16 6.35 us: cell_operator(): jnp.einsum('ij,jvc->ivc', face_jacobians[face_index], neighbor, precision...]
    concatenate x7 -> x0, local copies, waits for them, and re-layouts: 3.51 us -> none  [operate(): extended = jnp.concatenate([state_now] + incoming + [zero_block], axis=2)]
  transfers between devices with their start and end apart: 16 -> 0, of which waited for: 9 -> 0; matrix products, arithmetic and copies ran while one was open for 0% -> 0% of each run, Pallas kernels for 0% -> 0%
where the time goes in v1:
time: 59.1 us; the launch traced here: 58.9 us
  Pallas kernels  56.3 us (95%)
  local copies, waits for them, and re-layouts  1.31 us (2%)
  between operations  1.29 us (2%)
    pallas_call x1, Pallas kernels, shards(): pl.pallas_call(functools.partial(step_kernel, nx, ny), out_shape=(jax.Sha...  52.6 us
    pallas_call x1, Pallas kernels, shards(): pl.pallas_call(factor_kernel, out_shape=(jax.ShapeDtypeStruct((5, 64, 128...  3.68 us
    unnamed x1, local copies, waits for them, and re-layouts  1.31 us

profile of v1, /device:TPU:1, one launch (start us, length us, event | category | flops | bytes accessed | tf_op | source)
XLA Modules:
  0.0 58.9 jit_solution(4386678483853963033)
XLA Ops:
  1.3 1.3 %copy.10.fj_ref = f32[4,5,5]{2,1,0:T(8,128)} copy(f32[4,5,5]{2,0,1:T(4,128)} %param.9) | data formatting | bytes 800 | tf_op args[1]
  2.6 52.6 %advance_and_gram.1 = (f32[5,64,128]{2,1,0:T(8,128)}, f32[32,128]{1,0:T(8,128)}) custom-call(f32[5,64,128]{2,1,0:T(8,128)} %tv_ref.1, f32[4,5,5]{2,1,0:T(8,128)} %copy.10.fj_ref, f32[1,128]{1,0:T(1,128)} %bitcast.3, f32[1,128]{1,0:T(1,128)} %bitcast.4, f32[1,128]{1,0:T(1,128)} %bitcast.5, s32[4,128]{1,0:T(4,128)} %cn_ref.1, s32[4,16]{1,0:T(4,128)} %sr_ref.1, ...), custom_call_target="tpu_custom_call" | custom-call | tf_op jit(solution)/shard_map/advance_and_gram/pallas_call | solution.py:328
  55.2 3.7 %factor_and_apply.1 = (f32[5,64,128]{2,1,0:T(8,128)}, f32[64,64]{1,0:T(8,128)}) custom-call(f32[5,64,128]{2,1,0:T(8,128)} %get-tuple-element.4.adv_ref, f32[32,128]{1,0:T(8,128)} %get-tuple-element.5.gram_ref), custom_call_target="tpu_custom_call" | custom-call | tf_op jit(solution)/shard_map/factor_and_apply/pallas_call | solution.py:360

commit v2 on v1

--- a/solution.py
+++ b/solution.py
@@ -20,19 +20,27 @@
 def step_kernel(
     nx,
     ny,
-    tv_ref,
-    fj_ref,
-    ws_ref,
-    vi_ref,
-    iv_ref,
-    cn_ref,
-    sr_ref,
+    tv_hbm,
+    fj_hbm,
+    ws_hbm,
+    vi_hbm,
+    iv_hbm,
+    cn_hbm,
+    sr_hbm,
     cc_ref,
     adv_ref,
     gram_ref,
+    tv_ref,
+    fj_ref,
+    fac_ref,
+    cn_ref,
+    sr_ref,
+    load_sem,
     w_ref,
     acc_ref,
     pad_ref,
+    sidx_ref,
+    gidx_ref,
     send_ref,
     recv_ref,
     rows_ref,
@@ -41,6 +49,8 @@
     line_ref,
     done_ref,
     whole_ref,
+    met_x,
+    met_y,
     halo_send_sem,
     halo_recv_sem,
     scat_send_sem,
@@ -53,54 +63,74 @@
     gx = lax.axis_index("gx")
     gy = lax.axis_index("gy")
 
+    def around_x(o):
+        return (lax.rem(gx + o + nx, nx), gy)
+
+    def around_y(o):
+        return (gx, lax.rem(gy + o + ny, ny))
+
     barrier = pltpu.get_barrier_semaphore()
-
-    def greet_x(o, c):
-        pl.semaphore_signal(
-            barrier, inc=1, device_id=(lax.rem(gx + o, nx), gy), device_id_type=MESH
+    for there in (around_y(1), around_y(-1), around_x(1), around_x(-1)):
+        pl.semaphore_signal(barrier, inc=1, device_id=there, device_id_type=MESH)
+
+    loads = [
+        pltpu.make_async_copy(src, dst, load_sem.at[k])
+        for k, (src, dst) in enumerate(
+            (
+                (tv_hbm, tv_ref),
+                (fj_hbm, fj_ref),
+                (ws_hbm, fac_ref.at[0]),
+                (vi_hbm, fac_ref.at[1]),
+                (iv_hbm, fac_ref.at[2]),
+                (cn_hbm, cn_ref),
+                (sr_hbm, sr_ref),
+            )
         )
-        return c
-
-    def greet_y(o, c):
-        pl.semaphore_signal(
-            barrier, inc=1, device_id=(gx, lax.rem(gy + o, ny)), device_id_type=MESH
-        )
-        return c
-
-    lax.fori_loop(1, nx, greet_x, 0)
-    lax.fori_loop(1, ny, greet_y, 0)
+    ]
+    for k in (6, 5, 0, 2, 3, 4, 1):
+        loads[k].start()
 
     rows = lax.broadcasted_iota(jnp.int32, (64, 128), 0)
     lanes = lax.broadcasted_iota(jnp.int32, (64, 128), 1)
     lanes8 = lax.broadcasted_iota(jnp.int32, (8, 128), 1)
     group8 = lanes8 >> 4
     turn = ((lanes >> 4) - (rows >> 3)) & 7
-    listed = turn >> 1
-    spare = (turn & 1) == 1
+    base = (rows >> 3) << 4
 
     pad_ref[...] = jnp.zeros_like(pad_ref)
+    loads[6].wait()
     pad_ref[0:4, 0:16] = sr_ref[...]
     send_tile = pick(pad_ref[...], lanes8 & 15)
     send_idx = jnp.zeros((64, 128), jnp.int32)
     for k in range(4):
         row = jnp.broadcast_to(send_tile[k : k + 1, :], (64, 128))
-        send_idx = jnp.where(listed == k, row, send_idx)
-
-    a_row = -0.5 * ws_ref[...] * iv_ref[...]
-    b_row = vi_ref[...] * iv_ref[...]
-
+        send_idx = jnp.where((turn >> 1) == k, row, send_idx)
+    sidx_ref[...] = send_idx
+    loads[5].wait()
+    for f in range(4):
+        conn = jnp.broadcast_to(cn_ref[f : f + 1, :], (64, 128))
+        slot = conn - 128
+        there = base + (((slot >> 4) ^ 1) << 5) + (slot & 15)
+        ours = jnp.logical_and(conn >= 128, conn < 192)
+        gidx_ref[f] = jnp.where(ours, there, base + 16) & 127
+
+    for k in (0, 2, 3, 4, 1):
+        loads[k].wait()
+    a_row = -0.5 * fac_ref[0] * fac_ref[2]
+    b_row = fac_ref[1] * fac_ref[2]
     w_ref[...] = tv_ref[...]
 
-    pl.semaphore_wait(barrier, nx + ny - 2)
+    pl.semaphore_wait(barrier, 4)
 
     def halo(s, k):
         step = 1 if k % 2 else -1
         there = (gx + step, gy) if k < 2 else (gx, gy + step)
+        slot = lax.rem(s, 2)
         return pltpu.make_async_remote_copy(
-            src_ref=send_ref.at[s, k],
-            dst_ref=recv_ref.at[s, k],
-            send_sem=halo_send_sem.at[s, k],
-            recv_sem=halo_recv_sem.at[s, k],
+            src_ref=send_ref.at[slot, k],
+            dst_ref=recv_ref.at[slot, k],
+            send_sem=halo_send_sem.at[k],
+            recv_sem=halo_recv_sem.at[slot, k],
             device_id=there,
             device_id_type=MESH,
         )
@@ -108,26 +138,40 @@
     sends_to = [gx > 0, gx < nx - 1, gy > 0, gy < ny - 1]
     comes_in = [gx < nx - 1, gx > 0, gy < ny - 1, gy > 0]
 
+    def by_stage(s, values):
+        out = values[3]
+        for k in (2, 1, 0):
+            out = jnp.where(s == k, values[k], out)
+        return out
+
     def stage(s, carry):
-        scale = jnp.where(
-            s == 0,
-            F32(time_step / 4),
-            jnp.where(s == 1, F32(time_step / 3), jnp.where(s == 2, F32(time_step / 2), F32(time_step))),
-        )
+        scale = by_stage(s, [F32(time_step / 4), F32(time_step / 3), F32(time_step / 2), F32(time_step)])
         a_fac = jnp.broadcast_to(a_row * scale, (64, 128))
         b_fac = jnp.broadcast_to(b_row * scale, (64, 128))
         for j in range(5):
-            x = pick(w_ref[j], send_idx)
+            x = pick(w_ref[j], sidx_ref[...])
             for k in range(4):
                 out = x[0:8]
                 for g in range(1, 8):
                     out = jnp.where(group8 == (g + 2 * k) % 8, x[8 * g : 8 * g + 8], out)
-                send_ref[s, k, j] = out
+                send_ref[lax.rem(s, 2), k, j] = out
         for k in range(4):
 
             @pl.when(sends_to[k])
             def _(k=k):
                 halo(s, k).start()
+
+        @pl.when(s > 0)
+        def _():
+            pl.semaphore_wait(met_x.at[s - 1], 2)
+            pl.semaphore_wait(met_y.at[s - 1], 2)
+
+        far_x = by_stage(s, [d % nx for d in (1, 2, 4, 8)])
+        far_y = by_stage(s, [d % ny for d in (1, 2, 4, 8)])
+        for o in (far_x, nx - far_x):
+            pl.semaphore_signal(met_x.at[s], inc=1, device_id=around_x(o), device_id_type=MESH)
+        for o in (far_y, ny - far_y):
+            pl.semaphore_signal(met_y.at[s], inc=1, device_id=around_y(o), device_id_type=MESH)
 
         adv = [None] * 5
         dif = [None] * 5
@@ -139,10 +183,16 @@
                 n = jnp.where(own, pick(w_ref[j], idx), 0.0)
                 dif[j] = n if f == 0 else dif[j] + n
                 for i in range(5):
-                    t = fj_ref[f, i, j] * n
+                    t = fj_ref[i, f, j] * n
                     adv[i] = t if adv[i] is None else adv[i] + t
         for i in range(5):
             acc_ref[i] = tv_ref[i] + a_fac * adv[i] + b_fac * (dif[i] - 4.0 * w_ref[i])
+
+        for k in range(4):
+
+            @pl.when(sends_to[k])
+            def _(k=k):
+                halo(s, k).wait_send()
 
         for k in range(4):
 
@@ -155,19 +205,13 @@
         for j in range(5):
             ghost = jnp.zeros((64, 128), F32)
             for k in range(4):
-                block = jnp.concatenate([recv_ref[s, k, j]] * 8, axis=0)
-                ghost = jnp.where(jnp.logical_and(listed == k, jnp.logical_not(spare)), block, ghost)
+                block = jnp.concatenate([recv_ref[lax.rem(s, 2), k, j]] * 8, axis=0)
+                ghost = jnp.where(turn == 2 * k, block, ghost)
             for f in range(4):
-                conn = jnp.broadcast_to(cn_ref[f : f + 1, :], (64, 128))
-                slot = conn - 128
-                there = ((rows >> 3) << 4) + (((slot >> 4) ^ 1) << 5) + (slot & 15)
-                empty = ((rows >> 3) << 4) + 16
-                ours = jnp.logical_and(conn >= 128, conn < 192)
-                idx = jnp.where(ours, there, empty) & 127
-                n = pick(ghost, idx)
+                n = pick(ghost, gidx_ref[f])
                 dif[j] = n if f == 0 else dif[j] + n
                 for i in range(5):
-                    t = fj_ref[f, i, j] * n
+                    t = fj_ref[i, f, j] * n
                     adv[i] = t if adv[i] is None else adv[i] + t
         for i in range(5):
             w_ref[i] = acc_ref[i] + (a_fac * adv[i] + b_fac * dif[i])
@@ -187,25 +231,38 @@
     packed = jnp.where(lanes32 < 64, low, high)
     for r in range(32):
         rows_ref[r] = packed[r : r + 1]
+    pl.semaphore_wait(met_x.at[3], 2)
+    pl.semaphore_wait(met_y.at[3], 2)
 
     per = 32 // nx
-
-    def scatter(o):
-        to = lax.rem(gx + o, nx)
-        return pltpu.make_async_remote_copy(
+    wide = min(4, nx // 2)
+    high = nx // (2 * wide)
+    core = lax.rem(gx, 2)
+    col = lax.rem(gx // 2, wide)
+    row = gx // (2 * wide)
+    hops = lambda d, n: min(d, n - d)
+    partners = [
+        (dy, dx, dc) for dy in range(high) for dx in range(wide) for dc in range(2) if (dy, dx, dc) != (0, 0, 0)
+    ]
+    partners.sort(key=lambda d: -(2 * hops(d[0], high) + 2 * hops(d[1], wide) + d[2]))
+
+    def partner(dy, dx, dc):
+        there = (lax.rem(row + dy, high) * wide + lax.rem(col + dx, wide)) * 2 + lax.rem(core + dc, 2)
+        return there
+
+    def slot_of(dy, dx, dc):
+        return (((high - dy) % high) * wide + (wide - dx) % wide) * 2 + dc
+
+    for d in partners:
+        to = partner(*d)
+        pltpu.make_async_remote_copy(
             src_ref=rows_ref.at[pl.ds(to * per, per)],
-            dst_ref=part_ref.at[nx - o],
+            dst_ref=part_ref.at[slot_of(*d)],
             send_sem=scat_send_sem,
             recv_sem=scat_recv_sem,
             device_id=(to, gy),
             device_id_type=MESH,
-        )
-
-    def scatter_start(o, c):
-        scatter(o).start()
-        return c
-
-    lax.fori_loop(1, nx, scatter_start, 0)
+        ).start()
     part_ref[0] = rows_ref[pl.ds(gx * per, per)]
     sized = part_ref.at[pl.ds(1, nx - 1)]
     pltpu.make_async_copy(sized, sized, scat_recv_sem).wait()
@@ -214,21 +271,15 @@
         total = total + part_ref[o]
     mine_ref[...] = total
 
-    def line(o):
-        return pltpu.make_async_remote_copy(
+    for o in sorted(range(1, ny), key=lambda o: -hops(o, ny)):
+        pltpu.make_async_remote_copy(
             src_ref=mine_ref,
             dst_ref=line_ref.at[ny - o],
             send_sem=line_send_sem,
             recv_sem=line_recv_sem,
-            device_id=(gx, lax.rem(gy + o, ny)),
+            device_id=around_y(o),
             device_id_type=MESH,
-        )
-
-    def line_start(o, c):
-        line(o).start()
-        return c
-
-    lax.fori_loop(1, ny, line_start, 0)
+        ).start()
     line_ref[0] = total
     sized_line = line_ref.at[pl.ds(1, ny - 1)]
     pltpu.make_async_copy(sized_line, sized_line, line_recv_sem).wait()
@@ -238,33 +289,20 @@
     total = total / F32(5 * 128 * nx * ny)
     done_ref[...] = total
 
-    def gather(o):
-        return pltpu.make_async_remote_copy(
+    for d in partners:
+        pltpu.make_async_remote_copy(
             src_ref=done_ref,
             dst_ref=whole_ref.at[pl.ds(gx * per, per)],
             send_sem=gath_send_sem,
             recv_sem=gath_recv_sem,
-            device_id=(lax.rem(gx + o, nx), gy),
+            device_id=(partner(*d), gy),
             device_id_type=MESH,
-        )
-
-    def gather_start(o, c):
-        gather(o).start()
-        return c
-
-    lax.fori_loop(1, nx, gather_start, 0)
+        ).start()
     whole_ref[pl.ds(gx * per, per)] = total
     sized_whole = whole_ref.at[pl.ds(0, 32 - per)]
     pltpu.make_async_copy(sized_whole, sized_whole, gath_recv_sem).wait()
     for r in range(32):
         gram_ref[r : r + 1, :] = whole_ref[r]
-
-    for s in range(4):
-        for k in range(4):
-
-            @pl.when(sends_to[k])
-            def _(s=s, k=k):
-                halo(s, k).wait_send()
 
     pltpu.make_async_copy(sized, sized, scat_send_sem).wait()
     pltpu.make_async_copy(sized_line, sized_line, line_send_sem).wait()
@@ -323,30 +361,40 @@
     nx = lax.axis_size("gx")
     ny = lax.axis_size("gy")
     vmem = pl.BlockSpec(memory_space=pltpu.VMEM)
-    smem = pl.BlockSpec(memory_space=pltpu.SMEM)
     per = 32 // nx
+    hbm = pl.BlockSpec(memory_space=pltpu.HBM)
     adv, gram = pl.pallas_call(
         functools.partial(step_kernel, nx, ny),
         out_shape=(
             jax.ShapeDtypeStruct((5, 64, 128), F32),
             jax.ShapeDtypeStruct((32, 128), F32),
         ),
-        in_specs=[vmem, smem, vmem, vmem, vmem, vmem, vmem, smem],
+        in_specs=[hbm] * 7 + [pl.BlockSpec(memory_space=pltpu.SMEM)],
         out_specs=(vmem, vmem),
         scratch_shapes=[
             pltpu.VMEM((5, 64, 128), F32),
+            pltpu.SMEM((5, 4, 5), F32),
+            pltpu.VMEM((3, 1, 128), F32),
+            pltpu.VMEM((4, 128), jnp.int32),
+            pltpu.VMEM((4, 16), jnp.int32),
+            pltpu.SemaphoreType.DMA((7,)),
+            pltpu.VMEM((5, 64, 128), F32),
             pltpu.VMEM((5, 64, 128), F32),
             pltpu.VMEM((8, 128), jnp.int32),
-            pltpu.VMEM((4, 4, 5, 8, 128), F32),
-            pltpu.VMEM((4, 4, 5, 8, 128), F32),
+            pltpu.VMEM((64, 128), jnp.int32),
+            pltpu.VMEM((4, 64, 128), jnp.int32),
+            pltpu.VMEM((2, 4, 5, 8, 128), F32),
+            pltpu.VMEM((2, 4, 5, 8, 128), F32),
             pltpu.VMEM((32, 1, 128), F32),
             pltpu.VMEM((nx, per, 1, 128), F32),
             pltpu.VMEM((per, 1, 128), F32),
             pltpu.VMEM((ny, per, 1, 128), F32),
             pltpu.VMEM((per, 1, 128), F32),
             pltpu.VMEM((32, 1, 128), F32),
-            pltpu.SemaphoreType.DMA((4, 4)),
-            pltpu.SemaphoreType.DMA((4, 4)),
+            pltpu.SemaphoreType.REGULAR((4,)),
+            pltpu.SemaphoreType.REGULAR((4,)),
+            pltpu.SemaphoreType.DMA((4,)),
+            pltpu.SemaphoreType.DMA((2, 4)),
             pltpu.SemaphoreType.DMA,
             pltpu.SemaphoreType.DMA,
             pltpu.SemaphoreType.DMA,
@@ -354,9 +402,25 @@
             pltpu.SemaphoreType.DMA,
             pltpu.SemaphoreType.DMA,
         ],
-        compiler_params=pltpu.CompilerParams(collective_id=0, has_side_effects=True),
+        compiler_params=pltpu.CompilerParams(
+            collective_id=0, has_side_effects=True, vmem_limit_bytes=8 << 20
+        ),
         name="advance_and_gram",
-    )(tv, fj, ws.reshape(1, 128), vi.reshape(1, 128), iv.reshape(1, 128), cn, sr, cc)
+    )(
+        *[
+            pltpu.with_memory_space_constraint(v, pltpu.HBM)
+            for v in (
+                tv,
+                fj.transpose(1, 0, 2),
+                ws.reshape(1, 128),
+                vi.reshape(1, 128),
+                iv.reshape(1, 128),
+                cn,
+                sr,
+            )
+        ],
+        cc,
+    )
     return pl.pallas_call(
         factor_kernel,
         out_shape=(
@@ -365,6 +429,7 @@
         ),
         in_specs=[vmem, vmem],
         out_specs=(vmem, vmem),
+        compiler_params=pltpu.CompilerParams(vmem_limit_bytes=8 << 20),
         name="factor_and_apply",
     )(adv, gram)
 

time: 59.1 us -> 52.3 us (0.88)
  Pallas kernels: 56.3 us -> 50.9 us
  local copies, waits for them, and re-layouts: 1.31 us -> 0 us
    pallas_call x1, Pallas kernels: 52.6 us -> 48.1 us  [shards(): pl.pallas_call(functools.partial(step_kernel, nx, ny), out_shape=(jax.Sha...]
    unnamed x1 -> x0, local copies, waits for them, and re-layouts: 1.31 us -> none
    pallas_call x1, Pallas kernels: 3.68 us -> 2.76 us  [shards(): pl.pallas_call(factor_kernel, out_shape=(jax.ShapeDtypeStruct((5, 64, 128...]
where the time goes in v2:
time: 52.3 us; the launch traced here: 52.2 us
  Pallas kernels  50.9 us (97%)
  between operations  1.29 us (2%)
    pallas_call x1, Pallas kernels, shards(): pl.pallas_call(functools.partial(step_kernel, nx, ny), out_shape=(jax.Sha...  48.1 us
    pallas_call x1, Pallas kernels, shards(): pl.pallas_call(factor_kernel, out_shape=(jax.ShapeDtypeStruct((5, 64, 128...  2.76 us

profile of v2, /device:TPU:1, one launch (start us, length us, event | category | flops | bytes accessed | tf_op | source)
XLA Modules:
  0.0 52.2 jit_solution(4774875662504652020)
XLA Ops:
  1.3 48.1 %advance_and_gram.1 = (f32[5,64,128]{2,1,0:T(8,128)S(1)}, f32[32,128]{1,0:T(8,128)S(1)}) custom-call(f32[5,64,128]{2,1,0:T(8,128)} %tv_hbm.1, f32[5,4,5]{2,1,0:T(4,128)} %bitcast.4, f32[1,128]{1,0:T(1,128)} %bitcast.5, f32[1,128]{1,0:T(1,128)} %bitcast.6, f32[1,128]{1,0:T(1,128)} %bitcast.7, s32[4,128]{1,0:T(4,128)} %cn_hbm.1, s32[4,16]{1,0:T(4,128)} %sr_hbm.1, ...), custom_call_target="tpu_custom_call" | custom-call | tf_op jit(solution)/shard_map/advance_and_gram/pallas_call | solution.py:366
  49.4 2.8 %factor_and_apply.1 = (f32[5,64,128]{2,1,0:T(8,128)}, f32[64,64]{1,0:T(8,128)}) custom-call(f32[5,64,128]{2,1,0:T(8,128)S(1)} %get-tuple-element.4.adv_ref, f32[32,128]{1,0:T(8,128)S(1)} %get-tuple-element.5.gram_ref), custom_call_target="tpu_custom_call" | custom-call | tf_op jit(solution)/shard_map/factor_and_apply/pallas_call | solution.py:424

commit v3 on v2

--- a/solution.py
+++ b/solution.py
@@ -69,6 +69,11 @@
     def around_y(o):
         return (gx, lax.rem(gy + o + ny, ny))
 
+    block = 8 if nx == 32 else 4
+    high = nx // block
+    place = lax.rem(gx, block)
+    row = gx // block
+
     barrier = pltpu.get_barrier_semaphore()
     for there in (around_y(1), around_y(-1), around_x(1), around_x(-1)):
         pl.semaphore_signal(barrier, inc=1, device_id=there, device_id_type=MESH)
@@ -103,8 +108,8 @@
     send_tile = pick(pad_ref[...], lanes8 & 15)
     send_idx = jnp.zeros((64, 128), jnp.int32)
     for k in range(4):
-        row = jnp.broadcast_to(send_tile[k : k + 1, :], (64, 128))
-        send_idx = jnp.where((turn >> 1) == k, row, send_idx)
+        tiled = jnp.broadcast_to(send_tile[k : k + 1, :], (64, 128))
+        send_idx = jnp.where((turn >> 1) == k, tiled, send_idx)
     sidx_ref[...] = send_idx
     loads[5].wait()
     for f in range(4):
@@ -166,7 +171,7 @@
             pl.semaphore_wait(met_x.at[s - 1], 2)
             pl.semaphore_wait(met_y.at[s - 1], 2)
 
-        far_x = by_stage(s, [d % nx for d in (1, 2, 4, 8)])
+        far_x = by_stage(s, [d % nx for d in (1, 2, 4, block)])
         far_y = by_stage(s, [d % ny for d in (1, 2, 4, 8)])
         for o in (far_x, nx - far_x):
             pl.semaphore_signal(met_x.at[s], inc=1, device_id=around_x(o), device_id_type=MESH)
@@ -200,21 +205,28 @@
             def _(k=k):
                 halo(s, k).wait_recv()
 
-        adv = [None] * 5
-        dif = [None] * 5
-        for j in range(5):
-            ghost = jnp.zeros((64, 128), F32)
-            for k in range(4):
-                block = jnp.concatenate([recv_ref[lax.rem(s, 2), k, j]] * 8, axis=0)
-                ghost = jnp.where(turn == 2 * k, block, ghost)
+        for h in range(4):
+            at = pl.ds(16 * h, 16)
+            wheel = turn[16 * h : 16 * h + 16]
+            ghosts = []
+            for j in range(5):
+                ghost = jnp.zeros((16, 128), F32)
+                for k in range(4):
+                    one = recv_ref[lax.rem(s, 2), k, j]
+                    ghost = jnp.where(wheel == 2 * k, jnp.concatenate([one, one], axis=0), ghost)
+                ghosts.append(ghost)
+            adv = [None] * 5
+            dif = [None] * 5
             for f in range(4):
-                n = pick(ghost, gidx_ref[f])
-                dif[j] = n if f == 0 else dif[j] + n
-                for i in range(5):
-                    t = fj_ref[i, f, j] * n
-                    adv[i] = t if adv[i] is None else adv[i] + t
-        for i in range(5):
-            w_ref[i] = acc_ref[i] + (a_fac * adv[i] + b_fac * dif[i])
+                idx = gidx_ref[f, at]
+                for j in range(5):
+                    n = pick(ghosts[j], idx)
+                    dif[j] = n if f == 0 else dif[j] + n
+                    for i in range(5):
+                        t = fj_ref[i, f, j] * n
+                        adv[i] = t if adv[i] is None else adv[i] + t
+            for i in range(5):
+                w_ref[i, at] = acc_ref[i, at] + (a_fac[0:16] * adv[i] + b_fac[0:16] * dif[i])
         return carry
 
     lax.fori_loop(0, 4, stage, 0)
@@ -223,86 +235,83 @@
     adv = [jnp.where(live, w_ref[j], 0.0) for j in range(5)]
     for j in range(5):
         adv_ref[j] = adv[j]
-    flat = jnp.concatenate(adv, axis=1)
-    twice = jnp.concatenate([flat, flat], axis=0)
-    low = lax.dot_general(flat[0:32], twice, (((1,), (1,)), ((), ())), precision=HIGHEST, preferred_element_type=F32)
-    high = lax.dot_general(flat[32:64], twice, (((1,), (1,)), ((), ())), precision=HIGHEST, preferred_element_type=F32)
-    lanes32 = lax.broadcasted_iota(jnp.int32, (32, 128), 1)
-    packed = jnp.where(lanes32 < 64, low, high)
-    for r in range(32):
-        rows_ref[r] = packed[r : r + 1]
     pl.semaphore_wait(met_x.at[3], 2)
     pl.semaphore_wait(met_y.at[3], 2)
-
-    per = 32 // nx
-    wide = min(4, nx // 2)
-    high = nx // (2 * wide)
-    core = lax.rem(gx, 2)
-    col = lax.rem(gx // 2, wide)
-    row = gx // (2 * wide)
+    for o in (block, nx - block):
+        pl.semaphore_signal(met_x.at[4], inc=1, device_id=around_x(o), device_id_type=MESH)
+
+    flat = jnp.concatenate(adv, axis=1)
+    gram = lax.dot_general(flat, flat, (((1,), (1,)), ((), ())), precision=HIGHEST, preferred_element_type=F32)
+    packed = jnp.concatenate([gram[0:32], gram[32:64]], axis=1)
+    per = 32 // block
+    for r in range(block):
+        rows_ref[r] = packed[per * r : per * r + per]
+
     hops = lambda d, n: min(d, n - d)
-    partners = [
-        (dy, dx, dc) for dy in range(high) for dx in range(wide) for dc in range(2) if (dy, dx, dc) != (0, 0, 0)
-    ]
-    partners.sort(key=lambda d: -(2 * hops(d[0], high) + 2 * hops(d[1], wide) + d[2]))
-
-    def partner(dy, dx, dc):
-        there = (lax.rem(row + dy, high) * wide + lax.rem(col + dx, wide)) * 2 + lax.rem(core + dc, 2)
-        return there
-
-    def slot_of(dy, dx, dc):
-        return (((high - dy) % high) * wide + (wide - dx) % wide) * 2 + dc
-
-    for d in partners:
-        to = partner(*d)
+
+    def mate(o):
+        core = lax.rem(lax.rem(place, 2) + o, 2)
+        col = lax.rem(place // 2 + o // 2, block // 2)
+        return col * 2 + core
+
+    mates = sorted(range(1, block), key=lambda o: -hops(o // 2, block // 2))
+
+    for o in mates:
+        to = mate(o)
         pltpu.make_async_remote_copy(
-            src_ref=rows_ref.at[pl.ds(to * per, per)],
-            dst_ref=part_ref.at[slot_of(*d)],
+            src_ref=rows_ref.at[to],
+            dst_ref=part_ref.at[place],
             send_sem=scat_send_sem,
             recv_sem=scat_recv_sem,
-            device_id=(to, gy),
+            device_id=(row * block + to, gy),
             device_id_type=MESH,
         ).start()
-    part_ref[0] = rows_ref[pl.ds(gx * per, per)]
-    sized = part_ref.at[pl.ds(1, nx - 1)]
+    part_ref[place] = rows_ref[place]
+    sized = part_ref.at[pl.ds(1, block - 1)]
     pltpu.make_async_copy(sized, sized, scat_recv_sem).wait()
-    total = part_ref[0]
-    for o in range(1, nx):
-        total = total + part_ref[o]
+
+    def tree(parts):
+        while len(parts) > 1:
+            parts = [parts[k] + parts[k + 1] if k + 1 < len(parts) else parts[k] for k in range(0, len(parts), 2)]
+        return parts[0]
+
+    total = tree([part_ref[r] for r in range(block)])
     mine_ref[...] = total
-
-    for o in sorted(range(1, ny), key=lambda o: -hops(o, ny)):
+    pl.semaphore_wait(met_x.at[4], 2)
+
+    here = row * ny + gy
+    others = [(dy, dz) for dy in range(high) for dz in range(ny) if (dy, dz) != (0, 0)]
+    others.sort(key=lambda d: -hops(d[0], high) - hops(d[1], ny))
+    for dy, dz in others:
         pltpu.make_async_remote_copy(
             src_ref=mine_ref,
-            dst_ref=line_ref.at[ny - o],
+            dst_ref=line_ref.at[here],
             send_sem=line_send_sem,
             recv_sem=line_recv_sem,
-            device_id=around_y(o),
+            device_id=(lax.rem(row + dy, high) * block + place, lax.rem(gy + dz, ny)),
             device_id_type=MESH,
         ).start()
-    line_ref[0] = total
-    sized_line = line_ref.at[pl.ds(1, ny - 1)]
+    line_ref[here] = total
+    sized_line = line_ref.at[pl.ds(1, high * ny - 1)]
     pltpu.make_async_copy(sized_line, sized_line, line_recv_sem).wait()
-    total = line_ref[lax.rem(ny - gy, ny)]
-    for z in range(1, ny):
-        total = total + line_ref[lax.rem(ny + z - gy, ny)]
+    total = tree([line_ref[z] for z in range(high * ny)])
     total = total / F32(5 * 128 * nx * ny)
     done_ref[...] = total
 
-    for d in partners:
+    for o in mates:
         pltpu.make_async_remote_copy(
             src_ref=done_ref,
-            dst_ref=whole_ref.at[pl.ds(gx * per, per)],
+            dst_ref=whole_ref.at[place],
             send_sem=gath_send_sem,
             recv_sem=gath_recv_sem,
-            device_id=(partner(*d), gy),
+            device_id=(row * block + mate(o), gy),
             device_id_type=MESH,
         ).start()
-    whole_ref[pl.ds(gx * per, per)] = total
-    sized_whole = whole_ref.at[pl.ds(0, 32 - per)]
+    whole_ref[place] = total
+    sized_whole = whole_ref.at[pl.ds(1, block - 1)]
     pltpu.make_async_copy(sized_whole, sized_whole, gath_recv_sem).wait()
-    for r in range(32):
-        gram_ref[r : r + 1, :] = whole_ref[r]
+    for r in range(block):
+        gram_ref[per * r : per * r + per, :] = whole_ref[r]
 
     pltpu.make_async_copy(sized, sized, scat_send_sem).wait()
     pltpu.make_async_copy(sized_line, sized_line, line_send_sem).wait()
@@ -361,7 +370,8 @@
     nx = lax.axis_size("gx")
     ny = lax.axis_size("gy")
     vmem = pl.BlockSpec(memory_space=pltpu.VMEM)
-    per = 32 // nx
+    block = 8 if nx == 32 else 4
+    per = 32 // block
     hbm = pl.BlockSpec(memory_space=pltpu.HBM)
     adv, gram = pl.pallas_call(
         functools.partial(step_kernel, nx, ny),
@@ -385,13 +395,13 @@
             pltpu.VMEM((4, 64, 128), jnp.int32),
             pltpu.VMEM((2, 4, 5, 8, 128), F32),
             pltpu.VMEM((2, 4, 5, 8, 128), F32),
-            pltpu.VMEM((32, 1, 128), F32),
-            pltpu.VMEM((nx, per, 1, 128), F32),
-            pltpu.VMEM((per, 1, 128), F32),
-            pltpu.VMEM((ny, per, 1, 128), F32),
-            pltpu.VMEM((per, 1, 128), F32),
-            pltpu.VMEM((32, 1, 128), F32),
-            pltpu.SemaphoreType.REGULAR((4,)),
+            pltpu.VMEM((block, per, 128), F32),
+            pltpu.VMEM((block, per, 128), F32),
+            pltpu.VMEM((per, 128), F32),
+            pltpu.VMEM((nx // block * ny, per, 128), F32),
+            pltpu.VMEM((per, 128), F32),
+            pltpu.VMEM((block, per, 128), F32),
+            pltpu.SemaphoreType.REGULAR((5,)),
             pltpu.SemaphoreType.REGULAR((4,)),
             pltpu.SemaphoreType.DMA((4,)),
             pltpu.SemaphoreType.DMA((2, 4)),

time: 52.3 us -> 52.3 us (level)
  no operation moved by 1% of the time
where the time goes in v3:
time: 52.3 us; the launch traced here: 52.1 us
  Pallas kernels  50.8 us (97%)
  between operations  1.29 us (2%)
    pallas_call x1, Pallas kernels, shards(): pl.pallas_call(functools.partial(step_kernel, nx, ny), out_shape=(jax.Sha...  48.1 us
    pallas_call x1, Pallas kernels, shards(): pl.pallas_call(factor_kernel, out_shape=(jax.ShapeDtypeStruct((5, 64, 128...  2.76 us

profile of v3, /device:TPU:1, one launch (start us, length us, event | category | flops | bytes accessed | tf_op | source)
XLA Modules:
  0.0 52.1 jit_solution(18269008844738531582)
XLA Ops:
  1.3 48.1 %advance_and_gram.1 = (f32[5,64,128]{2,1,0:T(8,128)S(1)}, f32[32,128]{1,0:T(8,128)S(1)}) custom-call(f32[5,64,128]{2,1,0:T(8,128)} %tv_hbm.1, f32[5,4,5]{2,1,0:T(4,128)} %bitcast.4, f32[1,128]{1,0:T(1,128)} %bitcast.5, f32[1,128]{1,0:T(1,128)} %bitcast.6, f32[1,128]{1,0:T(1,128)} %bitcast.7, s32[4,128]{1,0:T(4,128)} %cn_hbm.1, s32[4,16]{1,0:T(4,128)} %sr_hbm.1, ...), custom_call_target="tpu_custom_call" | custom-call | tf_op jit(solution)/shard_map/advance_and_gram/pallas_call | solution.py:376
  49.4 2.8 %factor_and_apply.1 = (f32[5,64,128]{2,1,0:T(8,128)}, f32[64,64]{1,0:T(8,128)}) custom-call(f32[5,64,128]{2,1,0:T(8,128)S(1)} %get-tuple-element.4.adv_ref, f32[32,128]{1,0:T(8,128)S(1)} %get-tuple-element.5.gram_ref), custom_call_target="tpu_custom_call" | custom-call | tf_op jit(solution)/shard_map/factor_and_apply/pallas_call | solution.py:434

commit v4 on v3

--- a/solution.py
+++ b/solution.py
@@ -69,10 +69,13 @@
     def around_y(o):
         return (gx, lax.rem(gy + o + ny, ny))
 
-    block = 8 if nx == 32 else 4
-    high = nx // block
+    block = nx // 4
     place = lax.rem(gx, block)
     row = gx // block
+    pair = row // 2
+    odd = lax.rem(row, 2)
+    flip = pair + odd - 2 * pair * odd
+    member = flip * block + place
 
     barrier = pltpu.get_barrier_semaphore()
     for there in (around_y(1), around_y(-1), around_x(1), around_x(-1)):
@@ -235,39 +238,43 @@
     adv = [jnp.where(live, w_ref[j], 0.0) for j in range(5)]
     for j in range(5):
         adv_ref[j] = adv[j]
-    pl.semaphore_wait(met_x.at[3], 2)
-    pl.semaphore_wait(met_y.at[3], 2)
-    for o in (block, nx - block):
-        pl.semaphore_signal(met_x.at[4], inc=1, device_id=around_x(o), device_id_type=MESH)
-
     flat = jnp.concatenate(adv, axis=1)
     gram = lax.dot_general(flat, flat, (((1,), (1,)), ((), ())), precision=HIGHEST, preferred_element_type=F32)
     packed = jnp.concatenate([gram[0:32], gram[32:64]], axis=1)
-    per = 32 // block
-    for r in range(block):
+    team = 2 * block
+    per = 32 // team
+    for r in range(team):
         rows_ref[r] = packed[per * r : per * r + per]
+    pl.semaphore_wait(met_x.at[3], 2)
+    pl.semaphore_wait(met_y.at[3], 2)
 
     hops = lambda d, n: min(d, n - d)
 
-    def mate(o):
-        core = lax.rem(lax.rem(place, 2) + o, 2)
-        col = lax.rem(place // 2 + o // 2, block // 2)
-        return col * 2 + core
-
-    mates = sorted(range(1, block), key=lambda o: -hops(o // 2, block // 2))
-
-    for o in mates:
-        to = mate(o)
+    def mate(other, dx, dc):
+        core = lax.rem(lax.rem(place, 2) + dc, 2)
+        col = lax.rem(place // 2 + dx, block // 2)
+        at = col * 2 + core
+        to_row = row + 1 - 2 * odd if other else row
+        to_flip = 1 - flip if other else flip
+        return to_flip * block + at, (to_row * block + at, gy)
+
+    mates = [
+        (other, dx, dc) for other in range(2) for dx in range(block // 2) for dc in range(2) if (other, dx, dc) != (0, 0, 0)
+    ]
+    mates.sort(key=lambda d: -d[0] - hops(d[1], block // 2))
+
+    for d in mates:
+        to, there = mate(*d)
         pltpu.make_async_remote_copy(
             src_ref=rows_ref.at[to],
-            dst_ref=part_ref.at[place],
+            dst_ref=part_ref.at[member],
             send_sem=scat_send_sem,
             recv_sem=scat_recv_sem,
-            device_id=(row * block + to, gy),
+            device_id=there,
             device_id_type=MESH,
         ).start()
-    part_ref[place] = rows_ref[place]
-    sized = part_ref.at[pl.ds(1, block - 1)]
+    part_ref[member] = rows_ref[member]
+    sized = part_ref.at[pl.ds(1, team - 1)]
     pltpu.make_async_copy(sized, sized, scat_recv_sem).wait()
 
     def tree(parts):
@@ -275,42 +282,43 @@
             parts = [parts[k] + parts[k + 1] if k + 1 < len(parts) else parts[k] for k in range(0, len(parts), 2)]
         return parts[0]
 
-    total = tree([part_ref[r] for r in range(block)])
+    total = tree([part_ref[r] for r in range(team)])
     mine_ref[...] = total
-    pl.semaphore_wait(met_x.at[4], 2)
-
-    here = row * ny + gy
-    others = [(dy, dz) for dy in range(high) for dz in range(ny) if (dy, dz) != (0, 0)]
-    others.sort(key=lambda d: -hops(d[0], high) - hops(d[1], ny))
+
+    here = pair * ny + gy
+    others = [(dy, dz) for dy in range(2) for dz in range(ny) if (dy, dz) != (0, 0)]
+    others.sort(key=lambda d: -d[0] - hops(d[1], ny))
     for dy, dz in others:
+        to_row = 3 - row if dy else row
         pltpu.make_async_remote_copy(
             src_ref=mine_ref,
             dst_ref=line_ref.at[here],
             send_sem=line_send_sem,
             recv_sem=line_recv_sem,
-            device_id=(lax.rem(row + dy, high) * block + place, lax.rem(gy + dz, ny)),
+            device_id=(to_row * block + place, lax.rem(gy + dz, ny)),
             device_id_type=MESH,
         ).start()
     line_ref[here] = total
-    sized_line = line_ref.at[pl.ds(1, high * ny - 1)]
+    sized_line = line_ref.at[pl.ds(1, 2 * ny - 1)]
     pltpu.make_async_copy(sized_line, sized_line, line_recv_sem).wait()
-    total = tree([line_ref[z] for z in range(high * ny)])
+    total = tree([line_ref[z] for z in range(2 * ny)])
     total = total / F32(5 * 128 * nx * ny)
     done_ref[...] = total
 
-    for o in mates:
+    for d in mates:
+        to, there = mate(*d)
         pltpu.make_async_remote_copy(
             src_ref=done_ref,
-            dst_ref=whole_ref.at[place],
+            dst_ref=whole_ref.at[member],
             send_sem=gath_send_sem,
             recv_sem=gath_recv_sem,
-            device_id=(row * block + mate(o), gy),
+            device_id=there,
             device_id_type=MESH,
         ).start()
-    whole_ref[place] = total
-    sized_whole = whole_ref.at[pl.ds(1, block - 1)]
+    whole_ref[member] = total
+    sized_whole = whole_ref.at[pl.ds(1, team - 1)]
     pltpu.make_async_copy(sized_whole, sized_whole, gath_recv_sem).wait()
-    for r in range(block):
+    for r in range(team):
         gram_ref[per * r : per * r + per, :] = whole_ref[r]
 
     pltpu.make_async_copy(sized, sized, scat_send_sem).wait()
@@ -370,8 +378,9 @@
     nx = lax.axis_size("gx")
     ny = lax.axis_size("gy")
     vmem = pl.BlockSpec(memory_space=pltpu.VMEM)
-    block = 8 if nx == 32 else 4
-    per = 32 // block
+    block = nx // 4
+    team = 2 * block
+    per = 32 // team
     hbm = pl.BlockSpec(memory_space=pltpu.HBM)
     adv, gram = pl.pallas_call(
         functools.partial(step_kernel, nx, ny),
@@ -395,13 +404,13 @@
             pltpu.VMEM((4, 64, 128), jnp.int32),
             pltpu.VMEM((2, 4, 5, 8, 128), F32),
             pltpu.VMEM((2, 4, 5, 8, 128), F32),
-            pltpu.VMEM((block, per, 128), F32),
-            pltpu.VMEM((block, per, 128), F32),
+            pltpu.VMEM((team, per, 128), F32),
+            pltpu.VMEM((team, per, 128), F32),
             pltpu.VMEM((per, 128), F32),
-            pltpu.VMEM((nx // block * ny, per, 128), F32),
+            pltpu.VMEM((2 * ny, per, 128), F32),
             pltpu.VMEM((per, 128), F32),
-            pltpu.VMEM((block, per, 128), F32),
-            pltpu.SemaphoreType.REGULAR((5,)),
+            pltpu.VMEM((team, per, 128), F32),
+            pltpu.SemaphoreType.REGULAR((4,)),
             pltpu.SemaphoreType.REGULAR((4,)),
             pltpu.SemaphoreType.DMA((4,)),
             pltpu.SemaphoreType.DMA((2, 4)),

time: 52.3 us -> 50.3 us (0.962)
  Pallas kernels: 50.8 us -> 48.9 us
    pallas_call x1, Pallas kernels: 48.1 us -> 46.1 us  [shards(): pl.pallas_call(functools.partial(step_kernel, nx, ny), out_shape=(jax.Sha...]
where the time goes in v4:
time: 50.3 us; the launch traced here: 50.1 us
  Pallas kernels  48.9 us (97%)
  between operations  1.29 us (3%)
    pallas_call x1, Pallas kernels, shards(): pl.pallas_call(functools.partial(step_kernel, nx, ny), out_shape=(jax.Sha...  46.1 us
    pallas_call x1, Pallas kernels, shards(): pl.pallas_call(factor_kernel, out_shape=(jax.ShapeDtypeStruct((5, 64, 128...  2.76 us

profile of v4, /device:TPU:1, one launch (start us, length us, event | category | flops | bytes accessed | tf_op | source)
XLA Modules:
  0.0 50.1 jit_solution(6742358312200111677)
XLA Ops:
  1.3 46.1 %advance_and_gram.1 = (f32[5,64,128]{2,1,0:T(8,128)S(1)}, f32[32,128]{1,0:T(8,128)S(1)}) custom-call(f32[5,64,128]{2,1,0:T(8,128)} %tv_hbm.1, f32[5,4,5]{2,1,0:T(4,128)} %bitcast.4, f32[1,128]{1,0:T(1,128)} %bitcast.5, f32[1,128]{1,0:T(1,128)} %bitcast.6, f32[1,128]{1,0:T(1,128)} %bitcast.7, s32[4,128]{1,0:T(4,128)} %cn_hbm.1, s32[4,16]{1,0:T(4,128)} %sr_hbm.1, ...), custom_call_target="tpu_custom_call" | custom-call | tf_op jit(solution)/shard_map/advance_and_gram/pallas_call | solution.py:385
  47.4 2.8 %factor_and_apply.1 = (f32[5,64,128]{2,1,0:T(8,128)}, f32[64,64]{1,0:T(8,128)}) custom-call(f32[5,64,128]{2,1,0:T(8,128)S(1)} %get-tuple-element.4.adv_ref, f32[32,128]{1,0:T(8,128)S(1)} %get-tuple-element.5.gram_ref), custom_call_target="tpu_custom_call" | custom-call | tf_op jit(solution)/shard_map/factor_and_apply/pallas_call | solution.py:443

commit v5 on v4

--- a/solution.py
+++ b/solution.py
@@ -41,6 +41,7 @@
     pad_ref,
     sidx_ref,
     gidx_ref,
+    coef_ref,
     send_ref,
     recv_ref,
     rows_ref,
@@ -125,7 +126,13 @@
     for k in (0, 2, 3, 4, 1):
         loads[k].wait()
     a_row = -0.5 * fac_ref[0] * fac_ref[2]
-    b_row = fac_ref[1] * fac_ref[2]
+    ratio = jnp.broadcast_to(fac_ref[1] / (-0.5 * fac_ref[0]), (8, 128))
+    centre = jnp.broadcast_to(-4.0 * ratio[0:1], (64, 128))
+    for f in range(4):
+        for i in range(5):
+            for j in range(5):
+                entry = jnp.full((8, 128), fj_ref[i, f, j], F32)
+                coef_ref[f, i, j] = entry + ratio if i == j else entry
     w_ref[...] = tv_ref[...]
 
     pl.semaphore_wait(barrier, 4)
@@ -155,7 +162,6 @@
     def stage(s, carry):
         scale = by_stage(s, [F32(time_step / 4), F32(time_step / 3), F32(time_step / 2), F32(time_step)])
         a_fac = jnp.broadcast_to(a_row * scale, (64, 128))
-        b_fac = jnp.broadcast_to(b_row * scale, (64, 128))
         for j in range(5):
             x = pick(w_ref[j], sidx_ref[...])
             for k in range(4):
@@ -182,19 +188,17 @@
             pl.semaphore_signal(met_y.at[s], inc=1, device_id=around_y(o), device_id_type=MESH)
 
         adv = [None] * 5
-        dif = [None] * 5
         for f in range(4):
             conn = jnp.broadcast_to(cn_ref[f : f + 1, :], (64, 128))
             own = conn < 128
             idx = conn & 127
             for j in range(5):
                 n = jnp.where(own, pick(w_ref[j], idx), 0.0)
-                dif[j] = n if f == 0 else dif[j] + n
                 for i in range(5):
-                    t = fj_ref[i, f, j] * n
+                    t = jnp.concatenate([coef_ref[f, i, j]] * 8, axis=0) * n
                     adv[i] = t if adv[i] is None else adv[i] + t
         for i in range(5):
-            acc_ref[i] = tv_ref[i] + a_fac * adv[i] + b_fac * (dif[i] - 4.0 * w_ref[i])
+            acc_ref[i] = tv_ref[i] + a_fac * (adv[i] + centre * w_ref[i])
 
         for k in range(4):
 
@@ -208,28 +212,26 @@
             def _(k=k):
                 halo(s, k).wait_recv()
 
-        for h in range(4):
-            at = pl.ds(16 * h, 16)
-            wheel = turn[16 * h : 16 * h + 16]
+        for h in range(64 // 8):
+            at = pl.ds(8 * h, 8)
+            wheel = turn[8 * h : 8 * h + 8]
             ghosts = []
             for j in range(5):
-                ghost = jnp.zeros((16, 128), F32)
+                ghost = jnp.zeros((8, 128), F32)
                 for k in range(4):
-                    one = recv_ref[lax.rem(s, 2), k, j]
-                    ghost = jnp.where(wheel == 2 * k, jnp.concatenate([one, one], axis=0), ghost)
+                    block_of = jnp.concatenate([recv_ref[lax.rem(s, 2), k, j]] * (8 // 8), axis=0)
+                    ghost = jnp.where(wheel == 2 * k, block_of, ghost)
                 ghosts.append(ghost)
             adv = [None] * 5
-            dif = [None] * 5
             for f in range(4):
                 idx = gidx_ref[f, at]
                 for j in range(5):
                     n = pick(ghosts[j], idx)
-                    dif[j] = n if f == 0 else dif[j] + n
                     for i in range(5):
-                        t = fj_ref[i, f, j] * n
+                        t = jnp.concatenate([coef_ref[f, i, j]] * (8 // 8), axis=0) * n
                         adv[i] = t if adv[i] is None else adv[i] + t
             for i in range(5):
-                w_ref[i, at] = acc_ref[i, at] + (a_fac[0:16] * adv[i] + b_fac[0:16] * dif[i])
+                w_ref[i, at] = acc_ref[i, at] + a_fac[0:8] * adv[i]
         return carry
 
     lax.fori_loop(0, 4, stage, 0)
@@ -402,6 +404,7 @@
             pltpu.VMEM((8, 128), jnp.int32),
             pltpu.VMEM((64, 128), jnp.int32),
             pltpu.VMEM((4, 64, 128), jnp.int32),
+            pltpu.VMEM((4, 5, 5, 8, 128), F32),
             pltpu.VMEM((2, 4, 5, 8, 128), F32),
             pltpu.VMEM((2, 4, 5, 8, 128), F32),
             pltpu.VMEM((team, per, 128), F32),

time: 50.3 us -> 49.9 us (level)
  no operation moved by 1% of the time
where the time goes in v5:
time: 49.9 us; the launch traced here: 49.8 us
  Pallas kernels  48.5 us (97%)
  between operations  1.29 us (3%)
    pallas_call x1, Pallas kernels, shards(): pl.pallas_call(functools.partial(step_kernel, nx, ny), out_shape=(jax.Sha...  45.7 us
    pallas_call x1, Pallas kernels, shards(): pl.pallas_call(factor_kernel, out_shape=(jax.ShapeDtypeStruct((5, 64, 128...  2.76 us

profile of v5, /device:TPU:1, one launch (start us, length us, event | category | flops | bytes accessed | tf_op | source)
XLA Modules:
  0.0 49.8 jit_solution(15920117481931321195)
XLA Ops:
  1.3 45.7 %advance_and_gram.1 = (f32[5,64,128]{2,1,0:T(8,128)S(1)}, f32[32,128]{1,0:T(8,128)S(1)}) custom-call(f32[5,64,128]{2,1,0:T(8,128)} %tv_hbm.1, f32[5,4,5]{2,1,0:T(4,128)} %bitcast.4, f32[1,128]{1,0:T(1,128)} %bitcast.5, f32[1,128]{1,0:T(1,128)} %bitcast.6, f32[1,128]{1,0:T(1,128)} %bitcast.7, s32[4,128]{1,0:T(4,128)} %cn_hbm.1, s32[4,16]{1,0:T(4,128)} %sr_hbm.1, ...), custom_call_target="tpu_custom_call" | custom-call | tf_op jit(solution)/shard_map/advance_and_gram/pallas_call | solution.py:387
  47.0 2.8 %factor_and_apply.1 = (f32[5,64,128]{2,1,0:T(8,128)}, f32[64,64]{1,0:T(8,128)}) custom-call(f32[5,64,128]{2,1,0:T(8,128)S(1)} %get-tuple-element.4.adv_ref, f32[32,128]{1,0:T(8,128)S(1)} %get-tuple-element.5.gram_ref), custom_call_target="tpu_custom_call" | custom-call | tf_op jit(solution)/shard_map/factor_and_apply/pallas_call | solution.py:446

commit v6 on v5

--- a/solution.py
+++ b/solution.py
@@ -135,8 +135,6 @@
                 coef_ref[f, i, j] = entry + ratio if i == j else entry
     w_ref[...] = tv_ref[...]
 
-    pl.semaphore_wait(barrier, 4)
-
     def halo(s, k):
         step = 1 if k % 2 else -1
         there = (gx + step, gy) if k < 2 else (gx, gy + step)
@@ -162,13 +160,22 @@
     def stage(s, carry):
         scale = by_stage(s, [F32(time_step / 4), F32(time_step / 3), F32(time_step / 2), F32(time_step)])
         a_fac = jnp.broadcast_to(a_row * scale, (64, 128))
+        x = [[None] * 8 for _ in range(5)]
+        for g in range(8):
+            idx = sidx_ref[8 * g : 8 * g + 8]
+            for j in range(5):
+                x[j][g] = pick(w_ref[j, 8 * g : 8 * g + 8], idx)
         for j in range(5):
-            x = pick(w_ref[j], sidx_ref[...])
             for k in range(4):
-                out = x[0:8]
+                out = x[j][0]
                 for g in range(1, 8):
-                    out = jnp.where(group8 == (g + 2 * k) % 8, x[8 * g : 8 * g + 8], out)
+                    out = jnp.where(group8 == (g + 2 * k) % 8, x[j][g], out)
                 send_ref[lax.rem(s, 2), k, j] = out
+
+        @pl.when(s == 0)
+        def _():
+            pl.semaphore_wait(barrier, 4)
+
         for k in range(4):
 
             @pl.when(sends_to[k])

time: 49.9 us -> 49.7 us (level)
  no operation moved by 1% of the time
where the time goes in v6:
time: 49.7 us; the launch traced here: 49.5 us
  Pallas kernels  48.2 us (97%)
  between operations  1.29 us (3%)
    pallas_call x1, Pallas kernels, shards(): pl.pallas_call(functools.partial(step_kernel, nx, ny), out_shape=(jax.Sha...  45.5 us
    pallas_call x1, Pallas kernels, shards(): pl.pallas_call(factor_kernel, out_shape=(jax.ShapeDtypeStruct((5, 64, 128...  2.77 us

profile of v6, /device:TPU:1, one launch (start us, length us, event | category | flops | bytes accessed | tf_op | source)
XLA Modules:
  0.0 49.5 jit_solution(207016022436383054)
XLA Ops:
  1.3 45.5 %advance_and_gram.1 = (f32[5,64,128]{2,1,0:T(8,128)S(1)}, f32[32,128]{1,0:T(8,128)S(1)}) custom-call(f32[5,64,128]{2,1,0:T(8,128)} %tv_hbm.1, f32[5,4,5]{2,1,0:T(4,128)} %bitcast.4, f32[1,128]{1,0:T(1,128)} %bitcast.5, f32[1,128]{1,0:T(1,128)} %bitcast.6, f32[1,128]{1,0:T(1,128)} %bitcast.7, s32[4,128]{1,0:T(4,128)} %cn_hbm.1, s32[4,16]{1,0:T(4,128)} %sr_hbm.1, ...), custom_call_target="tpu_custom_call" | custom-call | tf_op jit(solution)/shard_map/advance_and_gram/pallas_call | solution.py:394
  46.8 2.8 %factor_and_apply.1 = (f32[5,64,128]{2,1,0:T(8,128)}, f32[64,64]{1,0:T(8,128)}) custom-call(f32[5,64,128]{2,1,0:T(8,128)S(1)} %get-tuple-element.4.adv_ref, f32[32,128]{1,0:T(8,128)S(1)} %get-tuple-element.5.gram_ref), custom_call_target="tpu_custom_call" | custom-call | tf_op jit(solution)/shard_map/factor_and_apply/pallas_call | solution.py:453

commit v7 on v6

--- a/solution.py
+++ b/solution.py
@@ -83,7 +83,7 @@
         pl.semaphore_signal(barrier, inc=1, device_id=there, device_id_type=MESH)
 
     loads = [
-        pltpu.make_async_copy(src, dst, load_sem.at[k])
+        pltpu.make_async_copy(src, dst, load_sem.at[(0, 1, 2, 2, 2, 3, 4)[k]])
         for k, (src, dst) in enumerate(
             (
                 (tv_hbm, tv_ref),
@@ -123,8 +123,9 @@
         ours = jnp.logical_and(conn >= 128, conn < 192)
         gidx_ref[f] = jnp.where(ours, there, base + 16) & 127
 
-    for k in (0, 2, 3, 4, 1):
-        loads[k].wait()
+    loads[0].wait()
+    loads[1].wait()
+    pltpu.make_async_copy(fac_ref, fac_ref, load_sem.at[2]).wait()
     a_row = -0.5 * fac_ref[0] * fac_ref[2]
     ratio = jnp.broadcast_to(fac_ref[1] / (-0.5 * fac_ref[0]), (8, 128))
     centre = jnp.broadcast_to(-4.0 * ratio[0:1], (64, 128))
@@ -184,8 +185,8 @@
 
         @pl.when(s > 0)
         def _():
-            pl.semaphore_wait(met_x.at[s - 1], 2)
-            pl.semaphore_wait(met_y.at[s - 1], 2)
+            pl.semaphore_wait(met_x.at[jnp.maximum(s - 1, 0)], 2)
+            pl.semaphore_wait(met_y.at[jnp.maximum(s - 1, 0)], 2)
 
         far_x = by_stage(s, [d % nx for d in (1, 2, 4, block)])
         far_y = by_stage(s, [d % ny for d in (1, 2, 4, 8)])
@@ -405,7 +406,7 @@
             pltpu.VMEM((3, 1, 128), F32),
             pltpu.VMEM((4, 128), jnp.int32),
             pltpu.VMEM((4, 16), jnp.int32),
-            pltpu.SemaphoreType.DMA((7,)),
+            pltpu.SemaphoreType.DMA((5,)),
             pltpu.VMEM((5, 64, 128), F32),
             pltpu.VMEM((5, 64, 128), F32),
             pltpu.VMEM((8, 128), jnp.int32),

time: 49.7 us -> 49.6 us (level)
  no operation moved by 1% of the time
where the time goes in v7:
time: 49.6 us; the launch traced here: 49.5 us
  Pallas kernels  48.2 us (97%)
  between operations  1.29 us (3%)
    pallas_call x1, Pallas kernels, shards(): pl.pallas_call(functools.partial(step_kernel, nx, ny), out_shape=(jax.Sha...  45.4 us
    pallas_call x1, Pallas kernels, shards(): pl.pallas_call(factor_kernel, out_shape=(jax.ShapeDtypeStruct((5, 64, 128...  2.76 us

profile of v7, /device:TPU:1, one launch (start us, length us, event | category | flops | bytes accessed | tf_op | source)
XLA Modules:
  0.0 49.5 jit_solution(16122383017616717356)
XLA Ops:
  1.3 45.4 %advance_and_gram.1 = (f32[5,64,128]{2,1,0:T(8,128)S(1)}, f32[32,128]{1,0:T(8,128)S(1)}) custom-call(f32[5,64,128]{2,1,0:T(8,128)} %tv_hbm.1, f32[5,4,5]{2,1,0:T(4,128)} %bitcast.4, f32[1,128]{1,0:T(1,128)} %bitcast.5, f32[1,128]{1,0:T(1,128)} %bitcast.6, f32[1,128]{1,0:T(1,128)} %bitcast.7, s32[4,128]{1,0:T(4,128)} %cn_hbm.1, s32[4,16]{1,0:T(4,128)} %sr_hbm.1, ...), custom_call_target="tpu_custom_call" | custom-call | tf_op jit(solution)/shard_map/advance_and_gram/pallas_call | solution.py:395
  46.7 2.8 %factor_and_apply.1 = (f32[5,64,128]{2,1,0:T(8,128)}, f32[64,64]{1,0:T(8,128)}) custom-call(f32[5,64,128]{2,1,0:T(8,128)S(1)} %get-tuple-element.4.adv_ref, f32[32,128]{1,0:T(8,128)S(1)} %get-tuple-element.5.gram_ref), custom_call_target="tpu_custom_call" | custom-call | tf_op jit(solution)/shard_map/factor_and_apply/pallas_call | solution.py:454
